TPU v7x, 256 devices: a whole 4x4x8 slice. The times are simulated.
256 devices in a mesh: seq: 32 (over x, z), head: 8 (over y, core).
Axes of the slice: x: 4, y: 4, z: 8, core: 2. Of those that a mesh axis runs over, the one named last changes fastest.
Arguments:
- cached_probs: bfloat16 [128, 40, 8, 128, 128], P('seq', 'head'), may hold values from 0 to 1, as said below
- out_old: bfloat16 [16384, 5120], P('seq', 'head'), may hold values from -6 to 6
- key_lists: int32 [128, 8], P('seq'), may hold values from 0 to 127, as said below
- changed_block_numbers: int32 [32], replicated, may hold values from 0 to 127, as said below
- delta_v: bfloat16 [4096, 1024], P('seq', 'head'), may hold values from -24 to 24
- w_out: bfloat16 [5120, 5120], P('head', 'seq'), may hold values from -0.078125 to 0.078125
Outputs:
- attn_new: bfloat16 [16384, 5120], P('seq', 'head')
- out_proj: bfloat16 [16384, 5120], P('seq', 'head')
Inputs may be any that keep to these rules, and one draw needn't show every extreme that they name: `changed_block_numbers`: the changed block numbers are all different; the first block and the last block are always among them. `key_lists`: each query block lists 8 different key blocks; some list many changed blocks, most list few. `cached_probs`: for each query block, head and row, the weights over the row's listed keys are positive and sum to at most 1.
All inputs are finite; a program needn't handle non-finite values.
Results may differ from a plain program's by a relative error of at most 0.017.
Values may be sent and summed in bfloat16 or wider, within the bound.
A program may use at most 128 MiB of HBM per device.

v0:
```python
import jax
import jax.numpy as jnp
from jax import lax
from jax.sharding import PartitionSpec as P

HD = 128
BLK = 128
GROUP = 5


def local(cached_probs, out_old, key_lists, changed_block_numbers, delta_v, w_out):
    blocks_here = cached_probs.shape[0]
    heads_here = cached_probs.shape[1]
    topk_here = cached_probs.shape[2]
    values_here = heads_here // GROUP
    change_rows = delta_v.reshape(delta_v.shape[0] // BLK, BLK * values_here * HD)
    flat_lists = key_lists.reshape(blocks_here * topk_here)
    every_change = lax.all_gather(change_rows, "seq", axis=0, tiled=True)
    onehot = (flat_lists[:, None] == changed_block_numbers[None, :]).astype(jnp.bfloat16)
    selected = jnp.dot(onehot, every_change, preferred_element_type=jnp.float32)
    picked = selected.astype(jnp.bfloat16).reshape(blocks_here, topk_here, BLK, values_here, HD)
    tiles = cached_probs.reshape(blocks_here, values_here, GROUP, topk_here, BLK, BLK)
    delta_out = jnp.einsum("qvgkij,qkjvd->qivgd", tiles, picked, preferred_element_type=jnp.float32)
    delta_out = delta_out.reshape(blocks_here * BLK, heads_here * HD)
    attn_new = (out_old.astype(jnp.float32) + delta_out).astype(jnp.bfloat16)
    terms = jnp.dot(
        attn_new,
        lax.all_gather(w_out, "seq", axis=1, tiled=True),
        preferred_element_type=jnp.float32,
    )
    out_proj = lax.psum_scatter(terms.astype(jnp.bfloat16), "head", scatter_dimension=1, tiled=True)
    return (attn_new, out_proj)


def solution(mesh):
    placed = (
        P("seq", "head", None, None, None),
        P("seq", "head"),
        P("seq", None),
        P(),
        P("seq", "head"),
        P("head", "seq"),
    )
    return jax.shard_map(
        local,
        mesh=mesh,
        in_specs=placed,
        out_specs=(P("seq", "head"), P("seq", "head")),
        check_vma=False,
    )
```

profile of v0, /device:TPU:2, one launch (start us, length us, event | category | flops | bytes accessed | tf_op | source)
XLA Modules:
  0.0 247.0 jit_solution(4615410390081621917)
XLA Ops:
  7.2 0.0 all-gather.6.cloned.1.call-start
  7.2 1.4 reshape.24
  8.6 0.0 all-gather.6.cloned.1.call-update
  8.6 0.0 all-gather.4.cloned.1.call-start
  8.7 0.7 all-gather.4.cloned.1.call-update
  9.4 0.0 copy-start.1
  9.4 0.0 copy-start
  9.4 0.0 copy-start.2
  9.4 0.0 reduce-scatter.4.cloned.1.call-start
  9.5 8.7 %copy.14 = bf16[4,5,8,128,128]{3,2,4,1,0:T(8,128)(2,1)} copy(bf16[4,5,8,128,128]{4,3,2,1,0:T(8,128)(2,1)} %param.6) | data formatting | bytes 10485760 | tf_op args[0]
  18.1 0.0 copy-done.1
  18.1 0.1 eq.15
  18.2 0.0 copy-done
  18.2 0.3 copy.13
  18.5 72.4 %all-gather.6.cloned.1.call-done = bf16[32,1,16384]{2,1,0:T(2,128)(2,1)} async-done(((bf16[1,1,16384]{2,1,0:T(2,128)(2,1)}), bf16[32,1,16384]{2,1,0:T(2,128)(2,1)}) %all-gather.6.cloned.1.call-update) | async-done | bytes 1048592 | tf_op jit(solution)/shard_map/all_gather | solution.py:18
  90.9 0.0 copy-done.2
  90.9 5.3 %convolution_bitcast_fusion = f32[4,128,1,5,128]{1,4,3,0,2:T(8,128)S(1)} fusion(bf16[4,5,8,128,128]{3,2,4,1,0:T(8,128)(2,1)} %copy.14, bf16[32,1,16384]{2,1,0:T(2,128)(2,1)} %all-gather.6.cloned.1.call-done, s32[32]{0:T(128)S(1)} %copy-done.2, s32[32]{0:T(128)S(1)} %eq.15), kind=kOutput, calls=%fused_computation.2 | convolution fusion | flops 705168384 | bytes 7602432 | tf_op jit(solution)/shard_map/qvgkij,qkjvd->qivgd/dot_general | solution.py:23
  96.2 0.8 copy.15
  97.1 0.3 fusion.1
  97.3 83.0 %all-gather.4.cloned.1.call-done = bf16[640,5120]{0,1:T(8,128)(2,1)} async-done(((bf16[640,160]{0,1:T(8,128)(2,1)}), bf16[640,5120]{0,1:T(8,128)(2,1)}) %all-gather.4.cloned.1.call-update) | async-done | bytes 6553616 | tf_op jit(solution)/shard_map/all_gather | solution.py:28
  180.3 8.9 %convolution_convert_fusion.1 = bf16[512,5120]{1,0:T(8,128)(2,1)} fusion(bf16[512,640]{0,1:T(8,128)(2,1)S(1)} %fusion.1, bf16[640,5120]{0,1:T(8,128)(2,1)} %all-gather.4.cloned.1.call-done), kind=kOutput, calls=%fused_computation.1 | convolution fusion | flops 3358064640 | bytes 12451840 | tf_op jit(solution)/shard_map/dot_general | solution.py:26
  189.3 7.9 %copy.19 = bf16[512,5120]{0,1:T(8,128)(2,1)} copy(bf16[512,5120]{1,0:T(8,128)(2,1)} %convolution_convert_fusion.1) | data formatting | bytes 10485760
  197.2 0.0 reduce-scatter.4.cloned.1.call-update
  197.2 1.1 copy.16
  198.3 40.0 %reduce-scatter.4.cloned.1.call-done = bf16[640,512]{1,0:T(8,128)(2,1)} async-done(((bf16[5120,512]{1,0:T(8,128)(2,1)}), bf16[640,512]{1,0:T(8,128)(2,1)}) %reduce-scatter.4.cloned.1.call-update) | async-done | bytes 655376
  238.3 2.2 copy.20
Async XLA Ops:
  7.2 83.7 %all-gather.6.cloned.1.call-start = ((), (), s32[]{:S(2)}) async-start(), calls=%async_computation.2 | async-start | bytes 2162688 | tf_op jit(solution)/shard_map/all_gather | solution.py:18
  8.6 171.7 %all-gather.4.cloned.1.call-start = ((), (), s32[]{:S(2)}) async-start(), calls=%async_computation.1 | async-start | bytes 6758400 | tf_op jit(solution)/shard_map/all_gather | solution.py:28
  9.4 8.7 %copy-start.1 = (s32[4,8]{1,0:T(4,128)S(1)}, s32[4,8]{1,0:T(4,128)}, u32[]{:S(2)}) copy-start(s32[4,8]{1,0:T(4,128)} %param.8) | copy-start | bytes 388
  9.4 8.8 %copy-start = (bf16[512,640]{1,0:T(8,128)(2,1)S(1)}, bf16[512,640]{1,0:T(8,128)(2,1)}, u32[]{:S(2)}) copy-start(bf16[512,640]{1,0:T(8,128)(2,1)} %param.7) | copy-start | bytes 1966084
  9.4 81.5 %copy-start.2 = (s32[32]{0:T(128)S(1)}, s32[32]{0:T(128)}, u32[]{:S(2)}) copy-start(s32[32]{0:T(128)} %param.9) | copy-start | bytes 388
  9.4 228.8 %reduce-scatter.4.cloned.1.call-start = ((), (), s32[]{:S(2)}) async-start(), calls=%async_computation.3 | async-start | bytes 5898240
Sparse Core Ops, SparseCore 0:
  11.2 79.6 all-gather.5
  93.5 86.8 all-gather.3
  197.3 40.8 reduce-scatter.3
where the time goes:
time: 248 us; the launch traced here: 247 us
  waiting for transfers between devices  196 us (79%)
  local copies, waits for them, and re-layouts  22.4 us (9%)
  matrix products  14.3 us (6%)
  between operations  13.8 us (6%)
    all_gather x1, waiting for transfers between devices, local(): lax.all_gather(w_out, 'seq', axis=1, tiled=True)  83 us
    all_gather x1, waiting for transfers between devices, local(): every_change = lax.all_gather(change_rows, 'seq', axis=0, tiled=True)  72.4 us
    unnamed x4, waiting for transfers between devices  40.7 us
    unnamed x12, local copies, waits for them, and re-layouts  21.5 us
    dot_general x1, matrix products, local(): jnp.dot(attn_new, lax.all_gather(w_out, 'seq', axis=1, tiled=True), prefe...  8.95 us
    dot_general x1, matrix products, local(): jnp.einsum('qvgkij,qkjvd->qivgd', tiles, picked, preferred_element_type=j...  5.33 us
  transfers between devices with their start and end apart: 3, of which 3 were waited for; matrix products, arithmetic and copies ran while one was open for 7% of the time, Pallas kernels for 0%

commit v1 on v0

v1 whole, which is shorter than its diff:
```python
import jax
import jax.numpy as jnp
from jax import lax
from jax.experimental import pallas as pl
from jax.experimental.pallas import tpu as pltpu
from jax.sharding import PartitionSpec as P

HD = 128
BLK = 128
GROUP = 5


def _gather_kernel(n, x_ref, o_ref, send_sem, recv_sem, local_sem):
    me = lax.axis_index("seq")
    hh = lax.axis_index("head")
    own = pltpu.make_async_copy(x_ref, o_ref.at[me], local_sem)
    own.start()
    copies = []
    for k in range(1, n):
        peer = lax.rem(me + k, n)
        copy = pltpu.make_async_remote_copy(
            src_ref=x_ref,
            dst_ref=o_ref.at[me],
            send_sem=send_sem.at[k],
            recv_sem=recv_sem.at[k],
            device_id=(peer, hh),
            device_id_type=pl.DeviceIdType.MESH,
        )
        copy.start()
        copies.append(copy)
    for copy in copies:
        copy.wait_send()
    for copy in copies:
        copy.wait_recv()
    own.wait()


def gather_seq(x, n):
    return pl.pallas_call(
        lambda *refs: _gather_kernel(n, *refs),
        out_shape=jax.ShapeDtypeStruct((n,) + x.shape, x.dtype),
        in_specs=[pl.BlockSpec(memory_space=pl.ANY)],
        out_specs=pl.BlockSpec(memory_space=pl.ANY),
        scratch_shapes=[
            pltpu.SemaphoreType.DMA((n,)),
            pltpu.SemaphoreType.DMA((n,)),
            pltpu.SemaphoreType.DMA,
        ],
        compiler_params=pltpu.CompilerParams(has_side_effects=True),
    )(x)


def local(n_seq, cached_probs, out_old, key_lists, changed_block_numbers, delta_v, w_out):
    blocks_here = cached_probs.shape[0]
    heads_here = cached_probs.shape[1]
    topk_here = cached_probs.shape[2]
    values_here = heads_here // GROUP
    w_full = lax.all_gather(w_out, "seq", axis=1, tiled=True)
    every_change = gather_seq(delta_v, n_seq)
    every_change = every_change.reshape(n_seq * delta_v.shape[0] // BLK, BLK * values_here * HD)
    flat_lists = key_lists.reshape(blocks_here * topk_here)
    onehot = (flat_lists[:, None] == changed_block_numbers[None, :]).astype(jnp.bfloat16)
    selected = jnp.dot(onehot, every_change, preferred_element_type=jnp.float32)
    picked = selected.astype(jnp.bfloat16).reshape(blocks_here, topk_here, BLK, values_here, HD)
    tiles = cached_probs.reshape(blocks_here, values_here, GROUP, topk_here, BLK, BLK)
    delta_out = jnp.einsum("qvgkij,qkjvd->qivgd", tiles, picked, preferred_element_type=jnp.float32)
    delta_out = delta_out.reshape(blocks_here * BLK, heads_here * HD)
    attn_new = (out_old.astype(jnp.float32) + delta_out).astype(jnp.bfloat16)
    terms = jnp.dot(attn_new, w_full, preferred_element_type=jnp.float32)
    out_proj = lax.psum_scatter(terms.astype(jnp.bfloat16), "head", scatter_dimension=1, tiled=True)
    return (attn_new, out_proj)


def solution(mesh):
    placed = (
        P("seq", "head", None, None, None),
        P("seq", "head"),
        P("seq", None),
        P(),
        P("seq", "head"),
        P("head", "seq"),
    )
    n_seq = mesh.shape["seq"]
    return jax.shard_map(
        lambda *a: local(n_seq, *a),
        mesh=mesh,
        in_specs=placed,
        out_specs=(P("seq", "head"), P("seq", "head")),
        check_vma=False,
    )
```

time: 248 us -> 177 us (0.71)
  waiting for transfers between devices: 196 us -> 79.7 us
  Pallas kernels: 0 us -> 47.8 us
    all_gather x2 -> x1, waiting for transfers between devices: 155 us -> 39.1 us  [local(): w_full = lax.all_gather(w_out, 'seq', axis=1, tiled=True)]
    pallas_call x0 -> x1, Pallas kernels: none -> 47.8 us  [gather_seq(): pl.pallas_call(lambda *refs: _gather_kernel(n, *refs), out_shape=jax.Shap...]
    unnamed x12 -> x11, local copies, waits for them, and re-layouts: 21.5 us -> 20.1 us
    unnamed x4 -> x3, waiting for transfers between devices: 40.7 us -> 40.7 us
  transfers between devices with their start and end apart: 3 -> 2, of which waited for: 3 -> 2; matrix products, arithmetic and copies ran while one was open for 7% -> 9% of each run, Pallas kernels for 0% -> 27%
where the time goes in v1:
time: 177 us; the launch traced here: 176 us
  waiting for transfers between devices  79.7 us (45%)
  Pallas kernels  47.8 us (27%)
  local copies, waits for them, and re-layouts  21 us (12%)
  between operations  14.1 us (8%)
  matrix products  13.4 us (8%)
    pallas_call x1, Pallas kernels, gather_seq(): pl.pallas_call(lambda *refs: _gather_kernel(n, *refs), out_shape=jax.Shap...  47.8 us
    unnamed x3, waiting for transfers between devices  40.7 us
    all_gather x1, waiting for transfers between devices, local(): w_full = lax.all_gather(w_out, 'seq', axis=1, tiled=True)  39.1 us
    unnamed x11, local copies, waits for them, and re-layouts  20.1 us
    dot_general x1, matrix products, local(): terms = jnp.dot(attn_new, w_full, preferred_element_type=jnp.float32)  8.93 us
    dot_general x1, matrix products, local(): jnp.einsum('qvgkij,qkjvd->qivgd', tiles, picked, preferred_element_type=j...  4.52 us
  transfers between devices with their start and end apart: 2, of which 2 were waited for; matrix products, arithmetic and copies ran while one was open for 9% of the time, Pallas kernels for 27%

profile of v1, /device:TPU:2, one launch (start us, length us, event | category | flops | bytes accessed | tf_op | source)
XLA Modules:
  0.0 176.5 jit_solution(7631536703260526931)
XLA Ops:
  7.2 0.0 all-gather.2.cloned.1.call-start
  7.2 0.7 all-gather.2.cloned.1.call-update
  7.9 0.0 copy-start.1
  7.9 0.0 copy-start.2
  7.9 0.0 reduce-scatter.4.cloned.1.call-start
  8.0 8.7 %copy.14 = bf16[4,5,8,128,128]{3,2,4,1,0:T(8,128)(2,1)} copy(bf16[4,5,8,128,128]{4,3,2,1,0:T(8,128)(2,1)} %param.6) | data formatting | bytes 10485760 | tf_op args[0]
  16.6 47.8 %shard_map.77 = bf16[32,128,128]{2,1,0:T(8,128)(2,1)} custom-call(bf16[128,128]{1,0:T(8,128)(2,1)} %refs_0_.1), custom_call_target="tpu_custom_call" | custom-call | tf_op jit(solution)/shard_map/pallas_call | solution.py:39
  64.4 0.0 copy-done.1
  64.5 0.0 copy-start
  64.5 0.1 eq.15
  64.6 0.0 copy-done.2
  64.6 4.5 %convolution_bitcast_fusion = f32[4,128,1,5,128]{1,4,3,0,2:T(8,128)S(1)} fusion(bf16[4,5,8,128,128]{3,2,4,1,0:T(8,128)(2,1)} %copy.14, bf16[4,8,128,128]{3,2,1,0:T(8,128)(2,1)} %bitcast.35, s32[32]{0:T(128)S(1)} %copy-done.2, s32[32]{0:T(128)S(1)} %eq.15), kind=kOutput, calls=%fused_computation.2 | convolution fusion | flops 705168384 | bytes 7602432 | tf_op jit(solution)/shard_map/qvgkij,qkjvd->qivgd/dot_general | solution.py:66
  69.1 0.8 copy.15
  69.9 0.0 copy-done
  69.9 0.3 copy.13
  70.2 0.3 fusion.1
  70.5 39.1 %all-gather.2.cloned.1.call-done = bf16[640,5120]{0,1:T(8,128)(2,1)} async-done(((bf16[640,160]{0,1:T(8,128)(2,1)}), bf16[640,5120]{0,1:T(8,128)(2,1)}) %all-gather.2.cloned.1.call-update) | async-done | bytes 6553616 | tf_op jit(solution)/shard_map/all_gather | solution.py:58
  109.5 8.9 %convolution_convert_fusion.1 = bf16[512,5120]{1,0:T(8,128)(2,1)} fusion(bf16[512,640]{0,1:T(8,128)(2,1)S(1)} %fusion.1, bf16[640,5120]{0,1:T(8,128)(2,1)} %all-gather.2.cloned.1.call-done), kind=kOutput, calls=%fused_computation.1 | convolution fusion | flops 3358064640 | bytes 12451840 | tf_op jit(solution)/shard_map/dot_general | solution.py:69
  118.5 7.9 %copy.19 = bf16[512,5120]{0,1:T(8,128)(2,1)} copy(bf16[512,5120]{1,0:T(8,128)(2,1)} %convolution_convert_fusion.1) | data formatting | bytes 10485760
  126.4 0.0 reduce-scatter.4.cloned.1.call-update
  126.4 1.1 copy.16
  127.5 40.0 %reduce-scatter.4.cloned.1.call-done = bf16[640,512]{1,0:T(8,128)(2,1)} async-done(((bf16[5120,512]{1,0:T(8,128)(2,1)}), bf16[640,512]{1,0:T(8,128)(2,1)}) %reduce-scatter.4.cloned.1.call-update) | async-done | bytes 655376
  167.5 2.2 %copy.20 = bf16[512,640]{1,0:T(8,128)(2,1)} copy(bf16[512,640]{0,1:T(8,128)(2,1)} %bitcast.36) | data formatting | bytes 1310720
Async XLA Ops:
  7.2 102.4 %all-gather.2.cloned.1.call-start = ((), (), s32[]{:S(2)}) async-start(), calls=%async_computation.1 | async-start | bytes 6758400 | tf_op jit(solution)/shard_map/all_gather | solution.py:58
  7.9 56.6 %copy-start.1 = (s32[4,8]{1,0:T(4,128)S(1)}, s32[4,8]{1,0:T(4,128)}, u32[]{:S(2)}) copy-start(s32[4,8]{1,0:T(4,128)} %param.8) | copy-start | bytes 388
  7.9 56.6 %copy-start.2 = (s32[32]{0:T(128)S(1)}, s32[32]{0:T(128)}, u32[]{:S(2)}) copy-start(s32[32]{0:T(128)} %param.9) | copy-start | bytes 388
  7.9 159.6 %reduce-scatter.4.cloned.1.call-start = ((), (), s32[]{:S(2)}) async-start(), calls=%async_computation.2 | async-start | bytes 5898240
  64.5 5.5 %copy-start = (bf16[512,640]{1,0:T(8,128)(2,1)S(1)}, bf16[512,640]{1,0:T(8,128)(2,1)}, u32[]{:S(2)}) copy-start(bf16[512,640]{1,0:T(8,128)(2,1)} %param.7) | copy-start | bytes 1966084
Sparse Core Ops, SparseCore 0:
  10.6 98.9 all-gather.1
  126.6 40.8 reduce-scatter.3

commit v2 on v1

--- a/solution.py
+++ b/solution.py
@@ -66,8 +66,10 @@
     delta_out = jnp.einsum("qvgkij,qkjvd->qivgd", tiles, picked, preferred_element_type=jnp.float32)
     delta_out = delta_out.reshape(blocks_here * BLK, heads_here * HD)
     attn_new = (out_old.astype(jnp.float32) + delta_out).astype(jnp.bfloat16)
-    terms = jnp.dot(attn_new, w_full, preferred_element_type=jnp.float32)
-    out_proj = lax.psum_scatter(terms.astype(jnp.bfloat16), "head", scatter_dimension=1, tiled=True)
+    n_head = w_full.shape[1] // attn_new.shape[1]
+    w_groups = w_full.reshape(w_full.shape[0], n_head, attn_new.shape[1])
+    terms = jnp.einsum("tk,kgc->gtc", attn_new, w_groups, preferred_element_type=jnp.float32)
+    out_proj = lax.psum_scatter(terms.astype(jnp.bfloat16), "head", scatter_dimension=0, tiled=True)[0]
     return (attn_new, out_proj)
 
 

time: 177 us -> 167 us (0.944)
  local copies, waits for them, and re-layouts: 21 us -> 10.9 us
    unnamed x3 -> x2, waiting for transfers between devices: 40.7 us -> 0.7 us
    reduce_scatter x0 -> x1, waiting for transfers between devices: none -> 40 us  [local(): lax.psum_scatter(terms.astype(jnp.bfloat16), 'head', scatter_dimension=0,...]
    unnamed x11 -> x9, local copies, waits for them, and re-layouts: 20.1 us -> 10 us
  transfers between devices with their start and end apart: 2 -> 2, of which waited for: 2 -> 2; matrix products, arithmetic and copies ran while one was open for 9% -> 9% of each run, Pallas kernels for 27% -> 29%
where the time goes in v2:
time: 167 us; the launch traced here: 166 us
  waiting for transfers between devices  79.7 us (48%)
  Pallas kernels  47.8 us (29%)
  between operations  14.1 us (8%)
  matrix products  13.4 us (8%)
  local copies, waits for them, and re-layouts  10.9 us (7%)
    pallas_call x1, Pallas kernels, gather_seq(): pl.pallas_call(lambda *refs: _gather_kernel(n, *refs), out_shape=jax.Shap...  47.8 us
    reduce_scatter x1, waiting for transfers between devices, local(): lax.psum_scatter(terms.astype(jnp.bfloat16), 'head', scatter_dimension=0,...  40 us
    all_gather x1, waiting for transfers between devices, local(): w_full = lax.all_gather(w_out, 'seq', axis=1, tiled=True)  39.1 us
    unnamed x9, local copies, waits for them, and re-layouts  10 us
    dot_general x1, matrix products, local(): jnp.einsum('tk,kgc->gtc', attn_new, w_groups, preferred_element_type=jnp....  8.91 us
    dot_general x1, matrix products, local(): jnp.einsum('qvgkij,qkjvd->qivgd', tiles, picked, preferred_element_type=j...  4.52 us
  transfers between devices with their start and end apart: 2, of which 2 were waited for; matrix products, arithmetic and copies ran while one was open for 9% of the time, Pallas kernels for 29%

profile of v2, /device:TPU:2, one launch (start us, length us, event | category | flops | bytes accessed | tf_op | source)
XLA Modules:
  0.0 166.4 jit_solution(6002988162551699467)
XLA Ops:
  7.2 0.0 all-gather.2.cloned.1.call-start
  7.2 0.7 all-gather.2.cloned.1.call-update
  7.9 0.0 copy-start.1
  7.9 0.0 copy-start.2
  7.9 0.0 reduce-scatter.2.cloned.1.call-start
  8.0 8.7 %copy.16 = bf16[4,5,8,128,128]{3,2,4,1,0:T(8,128)(2,1)} copy(bf16[4,5,8,128,128]{4,3,2,1,0:T(8,128)(2,1)} %param.6) | data formatting | bytes 10485760 | tf_op args[0]
  16.6 47.8 %shard_map.77 = bf16[32,128,128]{2,1,0:T(8,128)(2,1)} custom-call(bf16[128,128]{1,0:T(8,128)(2,1)} %refs_0_.1), custom_call_target="tpu_custom_call" | custom-call | tf_op jit(solution)/shard_map/pallas_call | solution.py:39
  64.4 0.0 copy-done.1
  64.5 0.0 copy-start
  64.5 0.1 eq.15
  64.6 0.0 copy-done.2
  64.6 4.5 %convolution_bitcast_fusion = f32[4,128,1,5,128]{1,4,3,0,2:T(8,128)S(1)} fusion(bf16[4,5,8,128,128]{3,2,4,1,0:T(8,128)(2,1)} %copy.16, bf16[4,8,128,128]{3,2,1,0:T(8,128)(2,1)} %bitcast.38, s32[32]{0:T(128)S(1)} %copy-done.2, s32[32]{0:T(128)S(1)} %eq.15), kind=kOutput, calls=%fused_computation.2 | convolution fusion | flops 705168384 | bytes 7602432 | tf_op jit(solution)/shard_map/qvgkij,qkjvd->qivgd/dot_general | solution.py:66
  69.1 0.8 copy.11
  69.9 0.0 copy-done
  69.9 0.3 copy.9
  70.2 0.3 fusion.1
  70.5 39.1 %all-gather.2.cloned.1.call-done = bf16[640,5120]{0,1:T(8,128)(2,1)} async-done(((bf16[640,160]{0,1:T(8,128)(2,1)}), bf16[640,5120]{0,1:T(8,128)(2,1)}) %all-gather.2.cloned.1.call-update) | async-done | bytes 6553616 | tf_op jit(solution)/shard_map/all_gather | solution.py:58
  109.5 8.9 %convert_bitcast_fusion = bf16[8,512,640]{2,1,0:T(8,128)(2,1)} fusion(bf16[640,8,640]{0,2,1:T(8,128)(2,1)} %bitcast.39, bf16[512,640]{0,1:T(8,128)(2,1)S(1)} %fusion.1), kind=kOutput, calls=%fused_computation.1 | convolution fusion | flops 3358064640 | bytes 12451840 | tf_op jit(solution)/shard_map/tk,kgc->gtc/dot_general | solution.py:71
  118.5 0.0 reduce-scatter.2.cloned.1.call-update
  118.5 1.1 copy.14
  119.6 40.0 %reduce-scatter.2.cloned.1.call-done = bf16[1,512,640]{2,1,0:T(8,128)(2,1)} async-done(((bf16[8,512,640]{2,1,0:T(8,128)(2,1)}), bf16[1,512,640]{2,1,0:T(8,128)(2,1)}) %reduce-scatter.2.cloned.1.call-update) | async-done | bytes 655376 | tf_op jit(solution)/shard_map/reduce_scatter | solution.py:72
Async XLA Ops:
  7.2 102.4 %all-gather.2.cloned.1.call-start = ((), (), s32[]{:S(2)}) async-start(), calls=%async_computation.1 | async-start | bytes 6758400 | tf_op jit(solution)/shard_map/all_gather | solution.py:58
  7.9 56.6 %copy-start.1 = (s32[4,8]{1,0:T(4,128)S(1)}, s32[4,8]{1,0:T(4,128)}, u32[]{:S(2)}) copy-start(s32[4,8]{1,0:T(4,128)} %param.8) | copy-start | bytes 388
  7.9 56.6 %copy-start.2 = (s32[32]{0:T(128)S(1)}, s32[32]{0:T(128)}, u32[]{:S(2)}) copy-start(s32[32]{0:T(128)} %param.9) | copy-start | bytes 388
  7.9 151.6 %reduce-scatter.2.cloned.1.call-start = ((), (), s32[]{:S(2)}) async-start(), calls=%async_computation.2 | async-start | bytes 5898240 | tf_op jit(solution)/shard_map/reduce_scatter | solution.py:72
  64.5 5.5 %copy-start = (bf16[512,640]{1,0:T(8,128)(2,1)S(1)}, bf16[512,640]{1,0:T(8,128)(2,1)}, u32[]{:S(2)}) copy-start(bf16[512,640]{1,0:T(8,128)(2,1)} %param.7) | copy-start | bytes 1966084
Sparse Core Ops, SparseCore 0:
  10.6 98.9 all-gather.1
  118.6 40.8 reduce-scatter.1

commit v3 on v1

--- a/solution.py
+++ b/solution.py
@@ -50,6 +50,37 @@
     )(x)
 
 
+def ring_reduce_scatter(attn_new, w_full):
+    n = w_full.shape[1] // attn_new.shape[1]
+    width = attn_new.shape[1]
+    rows = attn_new.shape[0]
+    half = rows // 2
+    me = lax.axis_index("head")
+    halves = (attn_new[:half], attn_new[half:])
+    shifts = (1, n - 1)
+
+    def partial(which, group):
+        cols = lax.dynamic_slice_in_dim(w_full, group * width, width, axis=1)
+        term = jnp.dot(halves[which], cols, preferred_element_type=jnp.float32)
+        return term.astype(jnp.bfloat16).astype(jnp.float32)
+
+    accs = []
+    for which in range(2):
+        sign = 1 if which == 0 else -1
+        accs.append(partial(which, lax.rem(me - sign + 2 * n, n)))
+    for step in range(n - 1):
+        sent = []
+        for which in range(2):
+            shift = shifts[which]
+            perm = [(i, (i + shift) % n) for i in range(n)]
+            sent.append(lax.ppermute(accs[which].astype(jnp.bfloat16), "head", perm))
+        for which in range(2):
+            sign = 1 if which == 0 else -1
+            group = lax.rem(me - sign * (step + 2) + 4 * n, n)
+            accs[which] = sent[which].astype(jnp.float32) + partial(which, group)
+    return jnp.concatenate([accs[0], accs[1]], axis=0).astype(jnp.bfloat16)
+
+
 def local(n_seq, cached_probs, out_old, key_lists, changed_block_numbers, delta_v, w_out):
     blocks_here = cached_probs.shape[0]
     heads_here = cached_probs.shape[1]
@@ -66,8 +97,7 @@
     delta_out = jnp.einsum("qvgkij,qkjvd->qivgd", tiles, picked, preferred_element_type=jnp.float32)
     delta_out = delta_out.reshape(blocks_here * BLK, heads_here * HD)
     attn_new = (out_old.astype(jnp.float32) + delta_out).astype(jnp.bfloat16)
-    terms = jnp.dot(attn_new, w_full, preferred_element_type=jnp.float32)
-    out_proj = lax.psum_scatter(terms.astype(jnp.bfloat16), "head", scatter_dimension=1, tiled=True)
+    out_proj = ring_reduce_scatter(attn_new, w_full)
     return (attn_new, out_proj)
 
 

time: 177 us -> 179 us (1.011); the launches traced: 176 us -> 177 us
  starting transfers between devices: 0.08 us -> 21.4 us
  waiting for transfers between devices: 79.7 us -> 62.6 us
  local copies, waits for them, and re-layouts: 21 us -> 10.9 us
  matrix products: 13.4 us -> 17.2 us
    unnamed x3 -> x1, waiting for transfers between devices: 40.7 us -> 0.68 us
    ppermute x0 -> x14, waiting for transfers between devices: none -> 24.2 us  [ring_reduce_scatter(): sent.append(lax.ppermute(accs[which].astype(jnp.bfloat16), 'head', perm))]
    ppermute x0 -> x14, starting transfers between devices: none -> 21.4 us  [ring_reduce_scatter(): sent.append(lax.ppermute(accs[which].astype(jnp.bfloat16), 'head', perm))]
    unnamed x11, local copies, waits for them, and re-layouts: 20.1 us -> 9.98 us
    dot_general x1 -> x16, matrix products: 8.93 us -> 12.7 us  [partial(): term = jnp.dot(halves[which], cols, preferred_element_type=jnp.float32)]
  transfers between devices with their start and end apart: 2 -> 15, of which waited for: 2 -> 13; matrix products, arithmetic and copies ran while one was open for 9% -> 15% of each run, Pallas kernels for 27% -> 27%
where the time goes in v3:
time: 179 us; the launch traced here: 177 us
  waiting for transfers between devices  62.6 us (35%)
  Pallas kernels  48.1 us (27%)
  starting transfers between devices  21.4 us (12%)
  matrix products  17.2 us (10%)
  between operations  14.4 us (8%)
  local copies, waits for them, and re-layouts  10.9 us (6%)
  other arithmetic  1.85 us (1%)
    pallas_call x1, Pallas kernels, gather_seq(): pl.pallas_call(lambda *refs: _gather_kernel(n, *refs), out_shape=jax.Shap...  48.1 us
    all_gather x1, waiting for transfers between devices, local(): w_full = lax.all_gather(w_out, 'seq', axis=1, tiled=True)  37.8 us
    ppermute x14, waiting for transfers between devices, ring_reduce_scatter(): sent.append(lax.ppermute(accs[which].astype(jnp.bfloat16), 'head', perm))  24.2 us
    ppermute x14, starting transfers between devices, ring_reduce_scatter(): sent.append(lax.ppermute(accs[which].astype(jnp.bfloat16), 'head', perm))  21.4 us
    dot_general x16, matrix products, partial(): term = jnp.dot(halves[which], cols, preferred_element_type=jnp.float32)  12.7 us
    unnamed x11, local copies, waits for them, and re-layouts  9.98 us
    dot_general x1, matrix products, local(): jnp.einsum('qvgkij,qkjvd->qivgd', tiles, picked, preferred_element_type=j...  4.47 us
  transfers between devices with their start and end apart: 15, of which 13 were waited for; matrix products, arithmetic and copies ran while one was open for 15% of the time, Pallas kernels for 27%

profile of v3, /device:TPU:2, one launch (start us, length us, event | category | flops | bytes accessed | tf_op | source)
XLA Modules:
  0.0 176.5 jit_solution(11863632768155347236)
XLA Ops:
  7.2 0.7 all-gather.2.cloned.1.call-update
  8.0 8.6 %copy.14 = bf16[4,5,8,128,128]{3,2,4,1,0:T(8,128)(2,1)} copy(bf16[4,5,8,128,128]{4,3,2,1,0:T(8,128)(2,1)} %param.6) | data formatting | bytes 10485760 | tf_op args[0]
  16.6 48.1 %shard_map.77 = bf16[32,128,128]{2,1,0:T(8,128)(2,1)} custom-call(bf16[128,128]{1,0:T(8,128)(2,1)} %refs_0_.1), custom_call_target="tpu_custom_call" | custom-call | tf_op jit(solution)/shard_map/pallas_call | solution.py:39
  64.9 4.5 %convolution_bitcast_fusion = f32[4,128,1,5,128]{1,4,3,0,2:T(8,128)S(1)} fusion(bf16[4,5,8,128,128]{3,2,4,1,0:T(8,128)(2,1)} %copy.14, bf16[4,8,128,128]{3,2,1,0:T(8,128)(2,1)} %bitcast.30, s32[32]{0:T(128)S(1)} %copy-done.3, s32[32]{0:T(128)S(1)} %eq.15), kind=kOutput, calls=%fused_computation.1 | convolution fusion | flops 705168384 | bytes 7602432 | tf_op jit(solution)/shard_map/qvgkij,qkjvd->qivgd/dot_general | solution.py:97
  69.3 0.8 copy.11
  70.7 1.1 copy.12
  71.8 37.8 %all-gather.2.cloned.1.call-done = bf16[640,5120]{0,1:T(8,128)(2,1)} async-done(((bf16[640,160]{0,1:T(8,128)(2,1)}), bf16[640,5120]{0,1:T(8,128)(2,1)}) %all-gather.2.cloned.1.call-update) | async-done | bytes 6553616 | tf_op jit(solution)/shard_map/all_gather | solution.py:89
  109.6 1.8 %convolution_convert_fusion.16 = bf16[256,640]{1,0:T(8,128)(2,1)S(1)} fusion(bf16[640,5120]{0,1:T(8,128)(2,1)} %all-gather.2.cloned.1.call-done, s32[]{:T(128)S(6)} %select_n.48, bf16[512,640]{0,1:T(8,128)(2,1)S(1)} %fusion.1), kind=kOutput, calls=%fused_computation.34 | convolution fusion | flops 209879040 | bytes 1474564 | tf_op jit(solution)/shard_map/dot_general | solution.py:64
  111.4 1.9 %convolution_convert_fusion.8 = bf16[256,640]{1,0:T(8,128)(2,1)S(1)} fusion(bf16[640,5120]{0,1:T(8,128)(2,1)} %all-gather.2.cloned.1.call-done, s32[]{:T(128)S(6)} %select_n.56, bf16[512,640]{0,1:T(8,128)(2,1)S(1)} %fusion.1), kind=kOutput, calls=%fused_computation.19 | convolution fusion | flops 209879040 | bytes 1474564 | tf_op jit(solution)/shard_map/dot_general | solution.py:64
  113.3 2.6 %collective-permute-start.7 = (bf16[256,640]{1,0:T(8,128)(2,1)S(1)}, bf16[256,640]{1,0:T(8,128)(2,1)S(1)}, u32[]{:S(2)}, u32[]{:S(2)}) collective-permute-start(bf16[256,640]{1,0:T(8,128)(2,1)S(1)} %convolution_convert_fusion.8), channel_id=1, source_target_pairs={{0,7},{1,0},{2,1},{3,2},{4,3},{5,4},{6,5},{7,6},{8,15},{9,8},{10,9... | collective-permute-start | bytes 983048 | tf_op jit(solution)/shard_map/ppermute | solution.py:76
  116.0 1.6 fusion.14
  117.6 1.6 fusion.13
  119.3 0.5 fusion.12
  119.7 0.5 fusion.11
  120.2 0.5 fusion.10
  120.7 0.5 fusion.9
  121.2 0.5 add_convert_fusion.13
  121.7 0.5 add_convert_fusion.6
  122.2 2.9 %collective-permute-start.8 = (bf16[256,640]{1,0:T(8,128)(2,1)S(1)}, bf16[256,640]{1,0:T(8,128)(2,1)S(1)}, u32[]{:S(2)}, u32[]{:S(2)}) collective-permute-start(bf16[256,640]{1,0:T(8,128)(2,1)S(1)} %add_convert_fusion.6), channel_id=1, source_target_pairs={{0,7},{1,0},{2,1},{3,2},{4,3},{5,4},{6,5},{7,6},{8,15},{9,8},{10,9... | collective-permute-start | bytes 983048 | tf_op jit(solution)/shard_map/ppermute | solution.py:76
  125.7 3.8 %collective-permute-done.1 = bf16[256,640]{1,0:T(8,128)(2,1)S(1)} collective-permute-done((bf16[256,640]{1,0:T(8,128)(2,1)S(1)}, bf16[256,640]{1,0:T(8,128)(2,1)S(1)}, u32[]{:S(2)}, u32[]{:S(2)}) %collective-permute-start.1) | collective-permute-done | bytes 327712 | tf_op jit(solution)/shard_map/ppermute | solution.py:76
  129.8 3.1 %collective-permute-start.9 = (bf16[256,640]{1,0:T(8,128)(2,1)S(1)}, bf16[256,640]{1,0:T(8,128)(2,1)S(1)}, u32[]{:S(2)}, u32[]{:S(2)}) collective-permute-start(bf16[256,640]{1,0:T(8,128)(2,1)S(1)} %add_convert_fusion.5), channel_id=1, source_target_pairs={{0,7},{1,0},{2,1},{3,2},{4,3},{5,4},{6,5},{7,6},{8,15},{9,8},{10,9... | collective-permute-start | bytes 983048 | tf_op jit(solution)/shard_map/ppermute | solution.py:76
  133.4 3.8 %collective-permute-done.2 = bf16[256,640]{1,0:T(8,128)(2,1)S(1)} collective-permute-done((bf16[256,640]{1,0:T(8,128)(2,1)S(1)}, bf16[256,640]{1,0:T(8,128)(2,1)S(1)}, u32[]{:S(2)}, u32[]{:S(2)}) %collective-permute-start.2) | collective-permute-done | bytes 327712 | tf_op jit(solution)/shard_map/ppermute | solution.py:76
  137.6 3.1 %collective-permute-start.10 = (bf16[256,640]{1,0:T(8,128)(2,1)S(1)}, bf16[256,640]{1,0:T(8,128)(2,1)S(1)}, u32[]{:S(2)}, u32[]{:S(2)}) collective-permute-start(bf16[256,640]{1,0:T(8,128)(2,1)S(1)} %add_convert_fusion.4), channel_id=1, source_target_pairs={{0,7},{1,0},{2,1},{3,2},{4,3},{5,4},{6,5},{7,6},{8,15},{9,8},{10,9... | collective-permute-start | bytes 983048 | tf_op jit(solution)/shard_map/ppermute | solution.py:76
  140.7 0.5 fusion.5
  141.2 3.8 %collective-permute-done.3 = bf16[256,640]{1,0:T(8,128)(2,1)S(1)} collective-permute-done((bf16[256,640]{1,0:T(8,128)(2,1)S(1)}, bf16[256,640]{1,0:T(8,128)(2,1)S(1)}, u32[]{:S(2)}, u32[]{:S(2)}) %collective-permute-start.3) | collective-permute-done | bytes 327712 | tf_op jit(solution)/shard_map/ppermute | solution.py:76
  145.4 3.1 %collective-permute-start.11 = (bf16[256,640]{1,0:T(8,128)(2,1)S(1)}, bf16[256,640]{1,0:T(8,128)(2,1)S(1)}, u32[]{:S(2)}, u32[]{:S(2)}) collective-permute-start(bf16[256,640]{1,0:T(8,128)(2,1)S(1)} %add_convert_fusion.3), channel_id=1, source_target_pairs={{0,7},{1,0},{2,1},{3,2},{4,3},{5,4},{6,5},{7,6},{8,15},{9,8},{10,9... | collective-permute-start | bytes 983048 | tf_op jit(solution)/shard_map/ppermute | solution.py:76
  149.0 3.8 %collective-permute-done.4 = bf16[256,640]{1,0:T(8,128)(2,1)S(1)} collective-permute-done((bf16[256,640]{1,0:T(8,128)(2,1)S(1)}, bf16[256,640]{1,0:T(8,128)(2,1)S(1)}, u32[]{:S(2)}, u32[]{:S(2)}) %collective-permute-start.4) | collective-permute-done | bytes 327712 | tf_op jit(solution)/shard_map/ppermute | solution.py:76
  153.2 3.1 %collective-permute-start.12 = (bf16[256,640]{1,0:T(8,128)(2,1)S(1)}, bf16[256,640]{1,0:T(8,128)(2,1)S(1)}, u32[]{:S(2)}, u32[]{:S(2)}) collective-permute-start(bf16[256,640]{1,0:T(8,128)(2,1)S(1)} %add_convert_fusion.2), channel_id=1, source_target_pairs={{0,7},{1,0},{2,1},{3,2},{4,3},{5,4},{6,5},{7,6},{8,15},{9,8},{10,9... | collective-permute-start | bytes 983048 | tf_op jit(solution)/shard_map/ppermute | solution.py:76
  156.8 3.8 %collective-permute-done.5 = bf16[256,640]{1,0:T(8,128)(2,1)S(1)} collective-permute-done((bf16[256,640]{1,0:T(8,128)(2,1)S(1)}, bf16[256,640]{1,0:T(8,128)(2,1)S(1)}, u32[]{:S(2)}, u32[]{:S(2)}) %collective-permute-start.5) | collective-permute-done | bytes 327712 | tf_op jit(solution)/shard_map/ppermute | solution.py:76
  161.0 3.1 %collective-permute-start.13 = (bf16[256,640]{1,0:T(8,128)(2,1)S(1)}, bf16[256,640]{1,0:T(8,128)(2,1)S(1)}, u32[]{:S(2)}, u32[]{:S(2)}) collective-permute-start(bf16[256,640]{1,0:T(8,128)(2,1)S(1)} %add_convert_fusion.1), channel_id=1, source_target_pairs={{0,7},{1,0},{2,1},{3,2},{4,3},{5,4},{6,5},{7,6},{8,15},{9,8},{10,9... | collective-permute-start | bytes 983048 | tf_op jit(solution)/shard_map/ppermute | solution.py:76
  164.6 3.8 %collective-permute-done.6 = bf16[256,640]{1,0:T(8,128)(2,1)S(1)} collective-permute-done((bf16[256,640]{1,0:T(8,128)(2,1)S(1)}, bf16[256,640]{1,0:T(8,128)(2,1)S(1)}, u32[]{:S(2)}, u32[]{:S(2)}) %collective-permute-start.6) | collective-permute-done | bytes 327712 | tf_op jit(solution)/shard_map/ppermute | solution.py:76
  168.8 0.9 pad_maximum_fusion
  (44 shorter events, 5.4 us)
Async XLA Ops:
  7.2 57.6 %copy-start.2 = (s32[4,8]{1,0:T(4,128)S(1)}, s32[4,8]{1,0:T(4,128)}, u32[]{:S(2)}) copy-start(s32[4,8]{1,0:T(4,128)} %param.8) | copy-start | bytes 388
  7.2 57.7 %copy-start.3 = (s32[32]{0:T(128)S(1)}, s32[32]{0:T(128)}, u32[]{:S(2)}) copy-start(s32[32]{0:T(128)} %param.9) | copy-start | bytes 388
  7.2 102.4 %all-gather.2.cloned.1.call-start = ((), (), s32[]{:S(2)}) async-start(), calls=%async_computation | async-start | bytes 6758400 | tf_op jit(solution)/shard_map/all_gather | solution.py:89
  16.6 53.5 %copy-start.1 = (bf16[512,640]{1,0:T(8,128)(2,1)S(1)}, bf16[512,640]{1,0:T(8,128)(2,1)}, u32[]{:S(2)}) copy-start(bf16[512,640]{1,0:T(8,128)(2,1)} %param.7) | copy-start | bytes 1966084
  109.6 9.7 %copy-start = (bf16[640,5120]{0,1:T(8,128)(2,1)S(1)}, bf16[640,5120]{0,1:T(8,128)(2,1)}, u32[]{:S(2)}) copy-start(bf16[640,5120]{0,1:T(8,128)(2,1)} %all-gather.2.cloned.1.call-done) | copy-start | bytes 19660804
  111.4 9.9 %collective-permute-start = (bf16[256,640]{1,0:T(8,128)(2,1)S(1)}, bf16[256,640]{1,0:T(8,128)(2,1)S(1)}, u32[]{:S(2)}, u32[]{:S(2)}) collective-permute-start(bf16[256,640]{1,0:T(8,128)(2,1)S(1)} %convolution_convert_fusion.16), channel_id=1, source_target_pairs={{0,1},{1,2},{2,3},{3,4},{4,5},{5,6},{6,7},{7,0},{8,9},{9,10},{10,1... | collective-permute-start | bytes 983048 | tf_op jit(solution)/shard_map/ppermute | solution.py:76
  113.3 8.4 %collective-permute-start.7 = (bf16[256,640]{1,0:T(8,128)(2,1)S(1)}, bf16[256,640]{1,0:T(8,128)(2,1)S(1)}, u32[]{:S(2)}, u32[]{:S(2)}) collective-permute-start(bf16[256,640]{1,0:T(8,128)(2,1)S(1)} %convolution_convert_fusion.8), channel_id=1, source_target_pairs={{0,7},{1,0},{2,1},{3,2},{4,3},{5,4},{6,5},{7,6},{8,15},{9,8},{10,9... | collective-permute-start | bytes 983048 | tf_op jit(solution)/shard_map/ppermute | solution.py:76
  121.7 7.7 %collective-permute-start.1 = (bf16[256,640]{1,0:T(8,128)(2,1)S(1)}, bf16[256,640]{1,0:T(8,128)(2,1)S(1)}, u32[]{:S(2)}, u32[]{:S(2)}) collective-permute-start(bf16[256,640]{1,0:T(8,128)(2,1)S(1)} %add_convert_fusion.13), channel_id=1, source_target_pairs={{0,1},{1,2},{2,3},{3,4},{4,5},{5,6},{6,7},{7,0},{8,9},{9,10},{10,1... | collective-permute-start | bytes 983048 | tf_op jit(solution)/shard_map/ppermute | solution.py:76
  122.2 7.5 %collective-permute-start.8 = (bf16[256,640]{1,0:T(8,128)(2,1)S(1)}, bf16[256,640]{1,0:T(8,128)(2,1)S(1)}, u32[]{:S(2)}, u32[]{:S(2)}) collective-permute-start(bf16[256,640]{1,0:T(8,128)(2,1)S(1)} %add_convert_fusion.6), channel_id=1, source_target_pairs={{0,7},{1,0},{2,1},{3,2},{4,3},{5,4},{6,5},{7,6},{8,15},{9,8},{10,9... | collective-permute-start | bytes 983048 | tf_op jit(solution)/shard_map/ppermute | solution.py:76
  129.5 7.7 %collective-permute-start.2 = (bf16[256,640]{1,0:T(8,128)(2,1)S(1)}, bf16[256,640]{1,0:T(8,128)(2,1)S(1)}, u32[]{:S(2)}, u32[]{:S(2)}) collective-permute-start(bf16[256,640]{1,0:T(8,128)(2,1)S(1)} %add_convert_fusion.12), channel_id=1, source_target_pairs={{0,1},{1,2},{2,3},{3,4},{4,5},{5,6},{6,7},{7,0},{8,9},{9,10},{10,1... | collective-permute-start | bytes 983048 | tf_op jit(solution)/shard_map/ppermute | solution.py:76
  129.8 7.7 %collective-permute-start.9 = (bf16[256,640]{1,0:T(8,128)(2,1)S(1)}, bf16[256,640]{1,0:T(8,128)(2,1)S(1)}, u32[]{:S(2)}, u32[]{:S(2)}) collective-permute-start(bf16[256,640]{1,0:T(8,128)(2,1)S(1)} %add_convert_fusion.5), channel_id=1, source_target_pairs={{0,7},{1,0},{2,1},{3,2},{4,3},{5,4},{6,5},{7,6},{8,15},{9,8},{10,9... | collective-permute-start | bytes 983048 | tf_op jit(solution)/shard_map/ppermute | solution.py:76
  137.3 7.7 %collective-permute-start.3 = (bf16[256,640]{1,0:T(8,128)(2,1)S(1)}, bf16[256,640]{1,0:T(8,128)(2,1)S(1)}, u32[]{:S(2)}, u32[]{:S(2)}) collective-permute-start(bf16[256,640]{1,0:T(8,128)(2,1)S(1)} %add_convert_fusion.11), channel_id=1, source_target_pairs={{0,1},{1,2},{2,3},{3,4},{4,5},{5,6},{6,7},{7,0},{8,9},{9,10},{10,1... | collective-permute-start | bytes 983048 | tf_op jit(solution)/shard_map/ppermute | solution.py:76
  137.6 7.7 %collective-permute-start.10 = (bf16[256,640]{1,0:T(8,128)(2,1)S(1)}, bf16[256,640]{1,0:T(8,128)(2,1)S(1)}, u32[]{:S(2)}, u32[]{:S(2)}) collective-permute-start(bf16[256,640]{1,0:T(8,128)(2,1)S(1)} %add_convert_fusion.4), channel_id=1, source_target_pairs={{0,7},{1,0},{2,1},{3,2},{4,3},{5,4},{6,5},{7,6},{8,15},{9,8},{10,9... | collective-permute-start | bytes 983048 | tf_op jit(solution)/shard_map/ppermute | solution.py:76
  145.1 7.7 %collective-permute-start.4 = (bf16[256,640]{1,0:T(8,128)(2,1)S(1)}, bf16[256,640]{1,0:T(8,128)(2,1)S(1)}, u32[]{:S(2)}, u32[]{:S(2)}) collective-permute-start(bf16[256,640]{1,0:T(8,128)(2,1)S(1)} %add_convert_fusion.10), channel_id=1, source_target_pairs={{0,1},{1,2},{2,3},{3,4},{4,5},{5,6},{6,7},{7,0},{8,9},{9,10},{10,1... | collective-permute-start | bytes 983048 | tf_op jit(solution)/shard_map/ppermute | solution.py:76
  145.4 7.7 %collective-permute-start.11 = (bf16[256,640]{1,0:T(8,128)(2,1)S(1)}, bf16[256,640]{1,0:T(8,128)(2,1)S(1)}, u32[]{:S(2)}, u32[]{:S(2)}) collective-permute-start(bf16[256,640]{1,0:T(8,128)(2,1)S(1)} %add_convert_fusion.3), channel_id=1, source_target_pairs={{0,7},{1,0},{2,1},{3,2},{4,3},{5,4},{6,5},{7,6},{8,15},{9,8},{10,9... | collective-permute-start | bytes 983048 | tf_op jit(solution)/shard_map/ppermute | solution.py:76
  152.8 7.7 %collective-permute-start.5 = (bf16[256,640]{1,0:T(8,128)(2,1)S(1)}, bf16[256,640]{1,0:T(8,128)(2,1)S(1)}, u32[]{:S(2)}, u32[]{:S(2)}) collective-permute-start(bf16[256,640]{1,0:T(8,128)(2,1)S(1)} %add_convert_fusion.9), channel_id=1, source_target_pairs={{0,1},{1,2},{2,3},{3,4},{4,5},{5,6},{6,7},{7,0},{8,9},{9,10},{10,1... | collective-permute-start | bytes 983048 | tf_op jit(solution)/shard_map/ppermute | solution.py:76
  153.2 7.7 %collective-permute-start.12 = (bf16[256,640]{1,0:T(8,128)(2,1)S(1)}, bf16[256,640]{1,0:T(8,128)(2,1)S(1)}, u32[]{:S(2)}, u32[]{:S(2)}) collective-permute-start(bf16[256,640]{1,0:T(8,128)(2,1)S(1)} %add_convert_fusion.2), channel_id=1, source_target_pairs={{0,7},{1,0},{2,1},{3,2},{4,3},{5,4},{6,5},{7,6},{8,15},{9,8},{10,9... | collective-permute-start | bytes 983048 | tf_op jit(solution)/shard_map/ppermute | solution.py:76
  160.6 7.7 %collective-permute-start.6 = (bf16[256,640]{1,0:T(8,128)(2,1)S(1)}, bf16[256,640]{1,0:T(8,128)(2,1)S(1)}, u32[]{:S(2)}, u32[]{:S(2)}) collective-permute-start(bf16[256,640]{1,0:T(8,128)(2,1)S(1)} %add_convert_fusion.8), channel_id=1, source_target_pairs={{0,1},{1,2},{2,3},{3,4},{4,5},{5,6},{6,7},{7,0},{8,9},{9,10},{10,1... | collective-permute-start | bytes 983048 | tf_op jit(solution)/shard_map/ppermute | solution.py:76
  161.0 7.7 %collective-permute-start.13 = (bf16[256,640]{1,0:T(8,128)(2,1)S(1)}, bf16[256,640]{1,0:T(8,128)(2,1)S(1)}, u32[]{:S(2)}, u32[]{:S(2)}) collective-permute-start(bf16[256,640]{1,0:T(8,128)(2,1)S(1)} %add_convert_fusion.1), channel_id=1, source_target_pairs={{0,7},{1,0},{2,1},{3,2},{4,3},{5,4},{6,5},{7,6},{8,15},{9,8},{10,9... | collective-permute-start | bytes 983048 | tf_op jit(solution)/shard_map/ppermute | solution.py:76
Sparse Core Ops, SparseCore 0:
  10.6 98.9 all-gather.1

commit v4 on v2

--- a/solution.py
+++ b/solution.py
@@ -10,54 +10,77 @@
 GROUP = 5
 
 
-def _gather_kernel(n, x_ref, o_ref, send_sem, recv_sem, local_sem):
+def _gather_kernel(nx, nz, x_ref, o_ref, send1, recv1, send2, recv2, local_sem):
     me = lax.axis_index("seq")
     hh = lax.axis_index("head")
+    mx = me // nz
+    mz = lax.rem(me, nz)
     own = pltpu.make_async_copy(x_ref, o_ref.at[me], local_sem)
     own.start()
-    copies = []
-    for k in range(1, n):
-        peer = lax.rem(me + k, n)
+    first = []
+    for k in range(1, nz):
+        peer = mx * nz + lax.rem(mz + k, nz)
         copy = pltpu.make_async_remote_copy(
             src_ref=x_ref,
             dst_ref=o_ref.at[me],
-            send_sem=send_sem.at[k],
-            recv_sem=recv_sem.at[k],
+            send_sem=send1.at[k],
+            recv_sem=recv1.at[k],
             device_id=(peer, hh),
             device_id_type=pl.DeviceIdType.MESH,
         )
         copy.start()
-        copies.append(copy)
-    for copy in copies:
+        first.append(copy)
+    own.wait()
+    for copy in first:
+        copy.wait_recv()
+    row = pl.ds(pl.multiple_of(mx * nz, nz), nz)
+    second = []
+    for k in range(1, nx):
+        peer = lax.rem(mx + k, nx) * nz + mz
+        copy = pltpu.make_async_remote_copy(
+            src_ref=o_ref.at[row],
+            dst_ref=o_ref.at[row],
+            send_sem=send2.at[k],
+            recv_sem=recv2.at[k],
+            device_id=(peer, hh),
+            device_id_type=pl.DeviceIdType.MESH,
+        )
+        copy.start()
+        second.append(copy)
+    for copy in first:
         copy.wait_send()
-    for copy in copies:
+    for copy in second:
+        copy.wait_send()
+    for copy in second:
         copy.wait_recv()
-    own.wait()
 
 
-def gather_seq(x, n):
+def gather_seq(x, nx, nz):
+    n = nx * nz
     return pl.pallas_call(
-        lambda *refs: _gather_kernel(n, *refs),
+        lambda *refs: _gather_kernel(nx, nz, *refs),
         out_shape=jax.ShapeDtypeStruct((n,) + x.shape, x.dtype),
         in_specs=[pl.BlockSpec(memory_space=pl.ANY)],
         out_specs=pl.BlockSpec(memory_space=pl.ANY),
         scratch_shapes=[
-            pltpu.SemaphoreType.DMA((n,)),
-            pltpu.SemaphoreType.DMA((n,)),
+            pltpu.SemaphoreType.DMA((nz,)),
+            pltpu.SemaphoreType.DMA((nz,)),
+            pltpu.SemaphoreType.DMA((nx,)),
+            pltpu.SemaphoreType.DMA((nx,)),
             pltpu.SemaphoreType.DMA,
         ],
         compiler_params=pltpu.CompilerParams(has_side_effects=True),
     )(x)
 
 
-def local(n_seq, cached_probs, out_old, key_lists, changed_block_numbers, delta_v, w_out):
+def local(nx, nz, cached_probs, out_old, key_lists, changed_block_numbers, delta_v, w_out):
     blocks_here = cached_probs.shape[0]
     heads_here = cached_probs.shape[1]
     topk_here = cached_probs.shape[2]
     values_here = heads_here // GROUP
     w_full = lax.all_gather(w_out, "seq", axis=1, tiled=True)
-    every_change = gather_seq(delta_v, n_seq)
-    every_change = every_change.reshape(n_seq * delta_v.shape[0] // BLK, BLK * values_here * HD)
+    every_change = gather_seq(delta_v, nx, nz)
+    every_change = every_change.reshape(nx * nz * delta_v.shape[0] // BLK, BLK * values_here * HD)
     flat_lists = key_lists.reshape(blocks_here * topk_here)
     onehot = (flat_lists[:, None] == changed_block_numbers[None, :]).astype(jnp.bfloat16)
     selected = jnp.dot(onehot, every_change, preferred_element_type=jnp.float32)
@@ -83,8 +106,9 @@
         P("head", "seq"),
     )
     n_seq = mesh.shape["seq"]
+    nz = 8 if n_seq % 8 == 0 else n_seq
     return jax.shard_map(
-        lambda *a: local(n_seq, *a),
+        lambda *a: local(n_seq // nz, nz, *a),
         mesh=mesh,
         in_specs=placed,
         out_specs=(P("seq", "head"), P("seq", "head")),

time: 167 us -> 163 us (0.976)
  Pallas kernels: 47.8 us -> 40.6 us
  waiting for transfers between devices: 79.7 us -> 83.5 us
    pallas_call x1, Pallas kernels: 47.8 us -> 40.6 us  [gather_seq(): pl.pallas_call(lambda *refs: _gather_kernel(nx, nz, *refs), out_shape=jax...]
    all_gather x1, waiting for transfers between devices: 39.1 us -> 42.8 us  [local(): w_full = lax.all_gather(w_out, 'seq', axis=1, tiled=True)]
  transfers between devices with their start and end apart: 2 -> 2, of which waited for: 2 -> 2; matrix products, arithmetic and copies ran while one was open for 9% -> 10% of each run, Pallas kernels for 29% -> 25%
where the time goes in v4:
time: 163 us
  waiting for transfers between devices  83.5 us (51%)
  Pallas kernels  40.6 us (25%)
  between operations  14.1 us (9%)
  matrix products  13.4 us (8%)
  local copies, waits for them, and re-layouts  10.9 us (7%)
    all_gather x1, waiting for transfers between devices, local(): w_full = lax.all_gather(w_out, 'seq', axis=1, tiled=True)  42.8 us
    pallas_call x1, Pallas kernels, gather_seq(): pl.pallas_call(lambda *refs: _gather_kernel(nx, nz, *refs), out_shape=jax...  40.6 us
    reduce_scatter x1, waiting for transfers between devices, local(): lax.psum_scatter(terms.astype(jnp.bfloat16), 'head', scatter_dimension=0,...  40 us
    unnamed x9, local copies, waits for them, and re-layouts  10 us
    dot_general x1, matrix products, local(): jnp.einsum('tk,kgc->gtc', attn_new, w_groups, preferred_element_type=jnp....  8.91 us
    dot_general x1, matrix products, local(): jnp.einsum('qvgkij,qkjvd->qivgd', tiles, picked, preferred_element_type=j...  4.52 us
  transfers between devices with their start and end apart: 2, of which 2 were waited for; matrix products, arithmetic and copies ran while one was open for 10% of the time, Pallas kernels for 25%

profile of v4, /device:TPU:2, one launch (start us, length us, event | category | flops | bytes accessed | tf_op | source)
XLA Modules:
  0.0 162.8 jit_solution(8547809291190113214)
XLA Ops:
  7.2 0.0 all-gather.2.cloned.1.call-start
  7.2 0.7 all-gather.2.cloned.1.call-update
  7.9 0.0 copy-start.1
  7.9 0.0 copy-start.2
  7.9 0.0 reduce-scatter.2.cloned.1.call-start
  8.0 8.7 %copy.16 = bf16[4,5,8,128,128]{3,2,4,1,0:T(8,128)(2,1)} copy(bf16[4,5,8,128,128]{4,3,2,1,0:T(8,128)(2,1)} %param.6) | data formatting | bytes 10485760 | tf_op args[0]
  16.6 40.6 %shard_map.77 = bf16[32,128,128]{2,1,0:T(8,128)(2,1)} custom-call(bf16[128,128]{1,0:T(8,128)(2,1)} %refs_0_.1), custom_call_target="tpu_custom_call" | custom-call | tf_op jit(solution)/shard_map/pallas_call | solution.py:60
  57.2 0.0 copy-done.1
  57.2 0.0 copy-start
  57.2 0.1 eq.15
  57.3 0.0 copy-done.2
  57.3 4.5 %convolution_bitcast_fusion = f32[4,128,1,5,128]{1,4,3,0,2:T(8,128)S(1)} fusion(bf16[4,5,8,128,128]{3,2,4,1,0:T(8,128)(2,1)} %copy.16, bf16[4,8,128,128]{3,2,1,0:T(8,128)(2,1)} %bitcast.38, s32[32]{0:T(128)S(1)} %copy-done.2, s32[32]{0:T(128)S(1)} %eq.15), kind=kOutput, calls=%fused_computation.2 | convolution fusion | flops 705168384 | bytes 7602432 | tf_op jit(solution)/shard_map/qvgkij,qkjvd->qivgd/dot_general | solution.py:89
  61.8 0.8 copy.11
  62.7 0.0 copy-done
  62.7 0.3 copy.9
  62.9 0.3 fusion.1
  63.2 42.8 %all-gather.2.cloned.1.call-done = bf16[640,5120]{0,1:T(8,128)(2,1)} async-done(((bf16[640,160]{0,1:T(8,128)(2,1)}), bf16[640,5120]{0,1:T(8,128)(2,1)}) %all-gather.2.cloned.1.call-update) | async-done | bytes 6553616 | tf_op jit(solution)/shard_map/all_gather | solution.py:81
  106.0 8.9 %convert_bitcast_fusion = bf16[8,512,640]{2,1,0:T(8,128)(2,1)} fusion(bf16[640,8,640]{0,2,1:T(8,128)(2,1)} %bitcast.39, bf16[512,640]{0,1:T(8,128)(2,1)S(1)} %fusion.1), kind=kOutput, calls=%fused_computation.1 | convolution fusion | flops 3358064640 | bytes 12451840 | tf_op jit(solution)/shard_map/tk,kgc->gtc/dot_general | solution.py:94
  114.9 0.0 reduce-scatter.2.cloned.1.call-update
  115.0 1.1 copy.14
  116.0 40.0 %reduce-scatter.2.cloned.1.call-done = bf16[1,512,640]{2,1,0:T(8,128)(2,1)} async-done(((bf16[8,512,640]{2,1,0:T(8,128)(2,1)}), bf16[1,512,640]{2,1,0:T(8,128)(2,1)}) %reduce-scatter.2.cloned.1.call-update) | async-done | bytes 655376 | tf_op jit(solution)/shard_map/reduce_scatter | solution.py:95
Async XLA Ops:
  7.2 98.9 %all-gather.2.cloned.1.call-start = ((), (), s32[]{:S(2)}) async-start(), calls=%async_computation.1 | async-start | bytes 6758400 | tf_op jit(solution)/shard_map/all_gather | solution.py:81
  7.9 49.3 %copy-start.1 = (s32[4,8]{1,0:T(4,128)S(1)}, s32[4,8]{1,0:T(4,128)}, u32[]{:S(2)}) copy-start(s32[4,8]{1,0:T(4,128)} %param.8) | copy-start | bytes 388
  7.9 49.4 %copy-start.2 = (s32[32]{0:T(128)S(1)}, s32[32]{0:T(128)}, u32[]{:S(2)}) copy-start(s32[32]{0:T(128)} %param.9) | copy-start | bytes 388
  7.9 148.1 %reduce-scatter.2.cloned.1.call-start = ((), (), s32[]{:S(2)}) async-start(), calls=%async_computation.2 | async-start | bytes 5898240 | tf_op jit(solution)/shard_map/reduce_scatter | solution.py:95
  57.2 5.5 %copy-start = (bf16[512,640]{1,0:T(8,128)(2,1)S(1)}, bf16[512,640]{1,0:T(8,128)(2,1)}, u32[]{:S(2)}) copy-start(bf16[512,640]{1,0:T(8,128)(2,1)} %param.7) | copy-start | bytes 1966084
Sparse Core Ops, SparseCore 0:
  10.6 95.4 all-gather.1
  115.1 40.8 reduce-scatter.1

commit v5 on v4

--- a/solution.py
+++ b/solution.py
@@ -73,6 +73,31 @@
     )(x)
 
 
+def _project_kernel(a_ref, w_ref, o_ref):
+    term = lax.dot_general(a_ref[...], w_ref[...], (((1,), (1,)), ((), ())), preferred_element_type=jnp.float32)
+    o_ref[0] = term.astype(o_ref.dtype)
+
+
+def project(a, w_t):
+    rows, width = a.shape
+    groups = w_t.shape[0] // width
+    return pl.pallas_call(
+        _project_kernel,
+        out_shape=jax.ShapeDtypeStruct((groups, rows, width), a.dtype),
+        grid=(groups,),
+        in_specs=[
+            pl.BlockSpec((rows, width), lambda g: (0, 0)),
+            pl.BlockSpec((width, w_t.shape[1]), lambda g: (g, 0)),
+        ],
+        out_specs=pl.BlockSpec((1, rows, width), lambda g: (g, 0, 0)),
+        cost_estimate=pl.CostEstimate(
+            flops=2 * rows * width * w_t.shape[0],
+            bytes_accessed=2 * (a.size + w_t.size + groups * rows * width),
+            transcendentals=0,
+        ),
+    )(a, w_t)
+
+
 def local(nx, nz, cached_probs, out_old, key_lists, changed_block_numbers, delta_v, w_out):
     blocks_here = cached_probs.shape[0]
     heads_here = cached_probs.shape[1]
@@ -89,9 +114,7 @@
     delta_out = jnp.einsum("qvgkij,qkjvd->qivgd", tiles, picked, preferred_element_type=jnp.float32)
     delta_out = delta_out.reshape(blocks_here * BLK, heads_here * HD)
     attn_new = (out_old.astype(jnp.float32) + delta_out).astype(jnp.bfloat16)
-    n_head = w_full.shape[1] // attn_new.shape[1]
-    w_groups = w_full.reshape(w_full.shape[0], n_head, attn_new.shape[1])
-    terms = jnp.einsum("tk,kgc->gtc", attn_new, w_groups, preferred_element_type=jnp.float32)
+    terms = project(attn_new, w_full.T)
     out_proj = lax.psum_scatter(terms.astype(jnp.bfloat16), "head", scatter_dimension=0, tiled=True)[0]
     return (attn_new, out_proj)
 

time: 163 us -> 165 us (1.012)
  Pallas kernels: 40.6 us -> 51 us
  matrix products: 13.4 us -> 4.47 us
  other arithmetic: 0.26 us -> 2.24 us
    pallas_call x0 -> x1, Pallas kernels: none -> 10.5 us  [project(): pl.pallas_call(_project_kernel, out_shape=jax.ShapeDtypeStruct((groups, r...]
    dot_general x1 -> x0, matrix products: 8.91 us -> none  [local(): jnp.einsum('tk,kgc->gtc', attn_new, w_groups, preferred_element_type=jnp....]
    convert_element_type x1, other arithmetic: 0.26 us -> 2.24 us  [local(): attn_new = (out_old.astype(jnp.float32) + delta_out).astype(jnp.bfloat16)]
    unnamed x9 -> x5, local copies, waits for them, and re-layouts: 10 us -> 8.65 us
where the time goes in v5:
time: 165 us; the launch traced here: 164 us
  waiting for transfers between devices  82.9 us (50%)
  Pallas kernels  51 us (31%)
  between operations  14.1 us (9%)
  local copies, waits for them, and re-layouts  9.64 us (6%)
  matrix products  4.47 us (3%)
  other arithmetic  2.24 us (1%)
    all_gather x1, waiting for transfers between devices, local(): w_full = lax.all_gather(w_out, 'seq', axis=1, tiled=True)  41.2 us
    reduce_scatter x1, waiting for transfers between devices, local(): lax.psum_scatter(terms.astype(jnp.bfloat16), 'head', scatter_dimension=0,...  41 us
    pallas_call x1, Pallas kernels, gather_seq(): pl.pallas_call(lambda *refs: _gather_kernel(nx, nz, *refs), out_shape=jax...  40.5 us
    pallas_call x1, Pallas kernels, project(): pl.pallas_call(_project_kernel, out_shape=jax.ShapeDtypeStruct((groups, r...  10.5 us
    unnamed x5, local copies, waits for them, and re-layouts  8.65 us
    dot_general x1, matrix products, local(): jnp.einsum('qvgkij,qkjvd->qivgd', tiles, picked, preferred_element_type=j...  4.47 us
  transfers between devices with their start and end apart: 2, of which 2 were waited for; matrix products, arithmetic and copies ran while one was open for 10% of the time, Pallas kernels for 25%

profile of v5, /device:TPU:2, one launch (start us, length us, event | category | flops | bytes accessed | tf_op | source)
XLA Modules:
  0.0 164.4 jit_solution(17985635919062499510)
XLA Ops:
  7.2 0.0 all-gather.2.cloned.1.call-start
  7.2 0.7 all-gather.2.cloned.1.call-update
  7.9 0.0 copy-start
  7.9 0.0 copy-start.1
  7.9 0.0 reduce-scatter.2.cloned.1.call-start
  8.0 8.6 %copy.14 = bf16[4,5,8,128,128]{3,2,4,1,0:T(8,128)(2,1)} copy(bf16[4,5,8,128,128]{4,3,2,1,0:T(8,128)(2,1)} %param.6) | data formatting | bytes 10485760 | tf_op args[0]
  16.6 40.5 %shard_map.77 = bf16[32,128,128]{2,1,0:T(8,128)(2,1)} custom-call(bf16[128,128]{1,0:T(8,128)(2,1)} %refs_0_.1), custom_call_target="tpu_custom_call" | custom-call | tf_op jit(solution)/shard_map/pallas_call | solution.py:60
  57.2 0.0 copy-done
  57.2 0.1 eq.15
  57.3 0.0 copy-done.1
  57.3 4.5 %convolution_bitcast_fusion = f32[4,128,1,5,128]{1,4,3,0,2:T(8,128)S(1)} fusion(bf16[4,5,8,128,128]{3,2,4,1,0:T(8,128)(2,1)} %copy.14, bf16[4,8,128,128]{3,2,1,0:T(8,128)(2,1)} %bitcast.32, s32[32]{0:T(128)S(1)} %copy-done.1, s32[32]{0:T(128)S(1)} %eq.15), kind=kOutput, calls=%fused_computation.1 | convolution fusion | flops 705168384 | bytes 7602432 | tf_op jit(solution)/shard_map/qvgkij,qkjvd->qivgd/dot_general | solution.py:114
  61.7 0.9 copy.18
  62.6 2.2 %fusion.1.a_ref = bf16[512,640]{1,0:T(8,128)(2,1)} fusion(f32[64,8,5,128]{3,2,1,0:T(8,128)S(1)} %bitcast.30, bf16[512,640]{1,0:T(8,128)(2,1)} %param.7), kind=kLoop, calls=%fused_computation.4 | loop fusion | flops 983040 | bytes 2621440 | tf_op jit(solution)/shard_map/convert_element_type | solution.py:116
  64.9 41.2 %all-gather.2.cloned.1.call-done = bf16[640,5120]{0,1:T(8,128)(2,1)} async-done(((bf16[640,160]{0,1:T(8,128)(2,1)}), bf16[640,5120]{0,1:T(8,128)(2,1)}) %all-gather.2.cloned.1.call-update) | async-done | bytes 6553616 | tf_op jit(solution)/shard_map/all_gather | solution.py:106
  106.1 10.5 %shard_map.78 = bf16[8,512,640]{2,1,0:T(8,128)(2,1)} custom-call(bf16[512,640]{1,0:T(8,128)(2,1)} %fusion.1.a_ref, bf16[5120,640]{1,0:T(8,128)(2,1)} %bitcast.31), custom_call_target="tpu_custom_call" | custom-call | flops 3355443200 | bytes 12451840 | tf_op jit(solution)/shard_map/pallas_call | solution.py:84
  116.5 0.0 reduce-scatter.2.cloned.1.call-update
  116.5 41.0 %reduce-scatter.2.cloned.1.call-done = bf16[1,512,640]{2,1,0:T(8,128)(2,1)} async-done(((bf16[8,512,640]{2,1,0:T(8,128)(2,1)}), bf16[1,512,640]{2,1,0:T(8,128)(2,1)}) %reduce-scatter.2.cloned.1.call-update) | async-done | bytes 655376 | tf_op jit(solution)/shard_map/reduce_scatter | solution.py:118
Async XLA Ops:
  7.2 98.9 %all-gather.2.cloned.1.call-start = ((), (), s32[]{:S(2)}) async-start(), calls=%async_computation.1 | async-start | bytes 6758400 | tf_op jit(solution)/shard_map/all_gather | solution.py:106
  7.9 49.3 %copy-start = (s32[4,8]{1,0:T(4,128)S(1)}, s32[4,8]{1,0:T(4,128)}, u32[]{:S(2)}) copy-start(s32[4,8]{1,0:T(4,128)} %param.8) | copy-start | bytes 388
  7.9 49.4 %copy-start.1 = (s32[32]{0:T(128)S(1)}, s32[32]{0:T(128)}, u32[]{:S(2)}) copy-start(s32[32]{0:T(128)} %param.9) | copy-start | bytes 388
  7.9 149.7 %reduce-scatter.2.cloned.1.call-start = ((), (), s32[]{:S(2)}) async-start(), calls=%async_computation.2 | async-start | bytes 5898240 | tf_op jit(solution)/shard_map/reduce_scatter | solution.py:118
Sparse Core Ops, SparseCore 0:
  10.6 95.4 all-gather.1
  116.7 40.8 reduce-scatter.1

commit v6 on v4

--- a/solution.py
+++ b/solution.py
@@ -80,6 +80,7 @@
     values_here = heads_here // GROUP
     w_full = lax.all_gather(w_out, "seq", axis=1, tiled=True)
     every_change = gather_seq(delta_v, nx, nz)
+    every_change, cached_probs = lax.optimization_barrier((every_change, cached_probs))
     every_change = every_change.reshape(nx * nz * delta_v.shape[0] // BLK, BLK * values_here * HD)
     flat_lists = key_lists.reshape(blocks_here * topk_here)
     onehot = (flat_lists[:, None] == changed_block_numbers[None, :]).astype(jnp.bfloat16)

time: 163 us -> 161 us (0.988)
  waiting for transfers between devices: 83.5 us -> 81.5 us
    optimization_barrier x0 -> x1, local copies, waits for them, and re-layouts: none -> 8.72 us  [local(): lax.optimization_barrier((every_change, cached_probs))]
    unnamed x9 -> x10, local copies, waits for them, and re-layouts: 10 us -> 1.35 us
    all_gather x1, waiting for transfers between devices: 42.8 us -> 40.9 us  [local(): w_full = lax.all_gather(w_out, 'seq', axis=1, tiled=True)]
where the time goes in v6:
time: 161 us; the launch traced here: 160 us
  waiting for transfers between devices  81.5 us (51%)
  Pallas kernels  40.2 us (25%)
  between operations  14.1 us (9%)
  matrix products  13.1 us (8%)
  local copies, waits for them, and re-layouts  11 us (7%)
    all_gather x1, waiting for transfers between devices, local(): w_full = lax.all_gather(w_out, 'seq', axis=1, tiled=True)  40.9 us
    pallas_call x1, Pallas kernels, gather_seq(): pl.pallas_call(lambda *refs: _gather_kernel(nx, nz, *refs), out_shape=jax...  40.2 us
    reduce_scatter x1, waiting for transfers between devices, local(): lax.psum_scatter(terms.astype(jnp.bfloat16), 'head', scatter_dimension=0,...  40 us
    dot_general x1, matrix products, local(): jnp.einsum('tk,kgc->gtc', attn_new, w_groups, preferred_element_type=jnp....  8.94 us
    optimization_barrier x1, local copies, waits for them, and re-layouts, local(): lax.optimization_barrier((every_change, cached_probs))  8.72 us
    dot_general x1, matrix products, local(): jnp.einsum('qvgkij,qkjvd->qivgd', tiles, picked, preferred_element_type=j...  4.19 us
  transfers between devices with their start and end apart: 2, of which 2 were waited for; matrix products, arithmetic and copies ran while one was open for 10% of the time, Pallas kernels for 25%

profile of v6, /device:TPU:2, one launch (start us, length us, event | category | flops | bytes accessed | tf_op | source)
XLA Modules:
  0.0 160.3 jit_solution(4073584731628536642)
XLA Ops:
  7.2 0.0 all-gather.2.cloned.1.call-start
  7.2 0.7 all-gather.2.cloned.1.call-update
  7.9 0.0 reduce-scatter.2.cloned.1.call-start
  7.9 40.2 %shard_map.77 = bf16[32,128,128]{2,1,0:T(8,128)(2,1)} custom-call(bf16[128,128]{1,0:T(8,128)(2,1)} %refs_0_.1), custom_call_target="tpu_custom_call" | custom-call | tf_op jit(solution)/shard_map/pallas_call | solution.py:60
  48.2 0.0 copy-start.2
  48.2 0.0 copy-start
  48.2 0.0 copy-start.3
  48.2 8.7 %copy.16 = bf16[4,5,8,128,128]{3,2,4,1,0:T(8,128)(2,1)} copy(bf16[4,5,8,128,128]{4,3,2,1,0:T(8,128)(2,1)} %param.6) | data formatting | bytes 10485760 | tf_op jit(solution)/shard_map/optimization_barrier | solution.py:83
  57.0 0.0 copy-done.2
  57.0 0.0 copy-start.1
  57.0 0.1 eq.15
  57.0 0.0 copy-done
  57.0 0.0 copy-done.3
  57.0 4.2 %convolution_bitcast_fusion = f32[4,128,1,5,128]{1,4,3,0,2:T(8,128)S(1)} fusion(bf16[4,5,8,128,128]{3,2,4,1,0:T(8,128)(2,1)} %copy.16, bf16[4,8,128,128]{3,2,1,0:T(8,128)(2,1)S(1)} %bitcast.38, s32[32]{0:T(128)S(1)} %copy-done.3, s32[32]{0:T(128)S(1)} %eq.15), kind=kOutput, calls=%fused_computation.2 | convolution fusion | flops 705168384 | bytes 7602432 | tf_op jit(solution)/shard_map/qvgkij,qkjvd->qivgd/dot_general | solution.py:90
  61.2 0.8 copy.11
  62.1 0.0 copy-done.1
  62.1 0.3 copy.9
  62.4 0.3 fusion.1
  62.6 40.9 %all-gather.2.cloned.1.call-done = bf16[640,5120]{0,1:T(8,128)(2,1)} async-done(((bf16[640,160]{0,1:T(8,128)(2,1)}), bf16[640,5120]{0,1:T(8,128)(2,1)}) %all-gather.2.cloned.1.call-update) | async-done | bytes 6553616 | tf_op jit(solution)/shard_map/all_gather | solution.py:81
  103.5 8.9 %convert_bitcast_fusion = bf16[8,512,640]{2,1,0:T(8,128)(2,1)} fusion(bf16[640,8,640]{0,2,1:T(8,128)(2,1)} %bitcast.39, bf16[512,640]{0,1:T(8,128)(2,1)S(1)} %fusion.1), kind=kOutput, calls=%fused_computation.1 | convolution fusion | flops 3358064640 | bytes 12451840 | tf_op jit(solution)/shard_map/tk,kgc->gtc/dot_general | solution.py:95
  112.4 0.0 reduce-scatter.2.cloned.1.call-update
  112.5 1.1 copy.14
  113.5 40.0 %reduce-scatter.2.cloned.1.call-done = bf16[1,512,640]{2,1,0:T(8,128)(2,1)} async-done(((bf16[8,512,640]{2,1,0:T(8,128)(2,1)}), bf16[1,512,640]{2,1,0:T(8,128)(2,1)}) %reduce-scatter.2.cloned.1.call-update) | async-done | bytes 655376 | tf_op jit(solution)/shard_map/reduce_scatter | solution.py:96
Async XLA Ops:
  7.2 96.3 %all-gather.2.cloned.1.call-start = ((), (), s32[]{:S(2)}) async-start(), calls=%async_computation.1 | async-start | bytes 6758400 | tf_op jit(solution)/shard_map/all_gather | solution.py:81
  7.9 145.6 %reduce-scatter.2.cloned.1.call-start = ((), (), s32[]{:S(2)}) async-start(), calls=%async_computation.2 | async-start | bytes 5898240 | tf_op jit(solution)/shard_map/reduce_scatter | solution.py:96
  48.2 8.8 %copy-start.2 = (s32[4,8]{1,0:T(4,128)S(1)}, s32[4,8]{1,0:T(4,128)}, u32[]{:S(2)}) copy-start(s32[4,8]{1,0:T(4,128)} %param.8) | copy-start | bytes 388
  48.2 8.8 %copy-start = (bf16[32,128,128]{2,1,0:T(8,128)(2,1)S(1)}, bf16[32,128,128]{2,1,0:T(8,128)(2,1)}, u32[]{:S(2)}) copy-start(bf16[32,128,128]{2,1,0:T(8,128)(2,1)} %shard_map.77) | copy-start | bytes 3145732
  48.2 8.8 %copy-start.3 = (s32[32]{0:T(128)S(1)}, s32[32]{0:T(128)}, u32[]{:S(2)}) copy-start(s32[32]{0:T(128)} %param.9) | copy-start | bytes 388
  57.0 5.1 %copy-start.1 = (bf16[512,640]{1,0:T(8,128)(2,1)S(1)}, bf16[512,640]{1,0:T(8,128)(2,1)}, u32[]{:S(2)}) copy-start(bf16[512,640]{1,0:T(8,128)(2,1)} %param.7) | copy-start | bytes 1966084
Sparse Core Ops, SparseCore 0:
  10.6 92.8 all-gather.1
  112.6 40.8 reduce-scatter.1

commit v7 on v6

--- a/solution.py
+++ b/solution.py
@@ -3,7 +3,7 @@
 from jax import lax
 from jax.experimental import pallas as pl
 from jax.experimental.pallas import tpu as pltpu
-from jax.sharding import PartitionSpec as P
+from jax.sharding import Mesh, PartitionSpec as P
 
 HD = 128
 BLK = 128
@@ -11,21 +11,21 @@
 
 
 def _gather_kernel(nx, nz, x_ref, o_ref, send1, recv1, send2, recv2, local_sem):
-    me = lax.axis_index("seq")
+    mx = lax.axis_index("sx")
+    mz = lax.axis_index("sz")
     hh = lax.axis_index("head")
-    mx = me // nz
-    mz = lax.rem(me, nz)
+    me = mx * nz + mz
     own = pltpu.make_async_copy(x_ref, o_ref.at[me], local_sem)
     own.start()
     first = []
     for k in range(1, nz):
-        peer = mx * nz + lax.rem(mz + k, nz)
+        peer = lax.rem(mz + k, nz)
         copy = pltpu.make_async_remote_copy(
             src_ref=x_ref,
             dst_ref=o_ref.at[me],
             send_sem=send1.at[k],
             recv_sem=recv1.at[k],
-            device_id=(peer, hh),
+            device_id=(mx, peer, hh),
             device_id_type=pl.DeviceIdType.MESH,
         )
         copy.start()
@@ -36,13 +36,13 @@
     row = pl.ds(pl.multiple_of(mx * nz, nz), nz)
     second = []
     for k in range(1, nx):
-        peer = lax.rem(mx + k, nx) * nz + mz
+        peer = lax.rem(mx + k, nx)
         copy = pltpu.make_async_remote_copy(
             src_ref=o_ref.at[row],
             dst_ref=o_ref.at[row],
             send_sem=send2.at[k],
             recv_sem=recv2.at[k],
-            device_id=(peer, hh),
+            device_id=(peer, mz, hh),
             device_id_type=pl.DeviceIdType.MESH,
         )
         copy.start()
@@ -53,6 +53,46 @@
         copy.wait_send()
     for copy in second:
         copy.wait_recv()
+
+
+def _gather_x_kernel(nx, x_ref, o_ref, send_sem, recv_sem, local_sem):
+    mx = lax.axis_index("sx")
+    mz = lax.axis_index("sz")
+    hh = lax.axis_index("head")
+    own = pltpu.make_async_copy(x_ref, o_ref.at[mx], local_sem)
+    own.start()
+    copies = []
+    for k in range(1, nx):
+        copy = pltpu.make_async_remote_copy(
+            src_ref=x_ref,
+            dst_ref=o_ref.at[mx],
+            send_sem=send_sem.at[k],
+            recv_sem=recv_sem.at[k],
+            device_id=(lax.rem(mx + k, nx), mz, hh),
+            device_id_type=pl.DeviceIdType.MESH,
+        )
+        copy.start()
+        copies.append(copy)
+    for copy in copies:
+        copy.wait_send()
+    for copy in copies:
+        copy.wait_recv()
+    own.wait()
+
+
+def gather_x(x, nx):
+    return pl.pallas_call(
+        lambda *refs: _gather_x_kernel(nx, *refs),
+        out_shape=jax.ShapeDtypeStruct((nx,) + x.shape, x.dtype),
+        in_specs=[pl.BlockSpec(memory_space=pl.ANY)],
+        out_specs=pl.BlockSpec(memory_space=pl.ANY),
+        scratch_shapes=[
+            pltpu.SemaphoreType.DMA((nx,)),
+            pltpu.SemaphoreType.DMA((nx,)),
+            pltpu.SemaphoreType.DMA,
+        ],
+        compiler_params=pltpu.CompilerParams(has_side_effects=True),
+    )(x)
 
 
 def gather_seq(x, nx, nz):
@@ -78,7 +118,7 @@
     heads_here = cached_probs.shape[1]
     topk_here = cached_probs.shape[2]
     values_here = heads_here // GROUP
-    w_full = lax.all_gather(w_out, "seq", axis=1, tiled=True)
+    w_rows = lax.all_gather(gather_x(w_out, nx), "sz", axis=0, tiled=False)
     every_change = gather_seq(delta_v, nx, nz)
     every_change, cached_probs = lax.optimization_barrier((every_change, cached_probs))
     every_change = every_change.reshape(nx * nz * delta_v.shape[0] // BLK, BLK * values_here * HD)
@@ -90,28 +130,34 @@
     delta_out = jnp.einsum("qvgkij,qkjvd->qivgd", tiles, picked, preferred_element_type=jnp.float32)
     delta_out = delta_out.reshape(blocks_here * BLK, heads_here * HD)
     attn_new = (out_old.astype(jnp.float32) + delta_out).astype(jnp.bfloat16)
-    n_head = w_full.shape[1] // attn_new.shape[1]
-    w_groups = w_full.reshape(w_full.shape[0], n_head, attn_new.shape[1])
-    terms = jnp.einsum("tk,kgc->gtc", attn_new, w_groups, preferred_element_type=jnp.float32)
+    width = attn_new.shape[1]
+    per_group = width // w_out.shape[1]
+    halves = nz // per_group
+    w_split = w_rows.reshape(halves, per_group, nx, w_out.shape[0], w_out.shape[1])
+    terms = jnp.einsum("tk,hlxkc->xhtlc", attn_new, w_split, preferred_element_type=jnp.float32)
+    terms = terms.reshape(nx * halves, attn_new.shape[0], width)
     out_proj = lax.psum_scatter(terms.astype(jnp.bfloat16), "head", scatter_dimension=0, tiled=True)[0]
     return (attn_new, out_proj)
 
 
 def solution(mesh):
-    placed = (
-        P("seq", "head", None, None, None),
-        P("seq", "head"),
-        P("seq", None),
-        P(),
-        P("seq", "head"),
-        P("head", "seq"),
-    )
     n_seq = mesh.shape["seq"]
     nz = 8 if n_seq % 8 == 0 else n_seq
+    nx = n_seq // nz
+    split = Mesh(mesh.devices.reshape(nx, nz, mesh.shape["head"]), ("sx", "sz", "head"))
+    seq = ("sx", "sz")
+    placed = (
+        P(seq, "head", None, None, None),
+        P(seq, "head"),
+        P(seq, None),
+        P(),
+        P(seq, "head"),
+        P("head", seq),
+    )
     return jax.shard_map(
-        lambda *a: local(n_seq // nz, nz, *a),
-        mesh=mesh,
+        lambda *a: local(nx, nz, *a),
+        mesh=split,
         in_specs=placed,
-        out_specs=(P("seq", "head"), P("seq", "head")),
+        out_specs=(P(seq, "head"), P(seq, "head")),
         check_vma=False,
     )

time: 161 us -> 186 us (1.16)
  Pallas kernels: 40.2 us -> 74.5 us
  waiting for transfers between devices: 81.5 us -> 65.3 us
  local copies, waits for them, and re-layouts: 11 us -> 20.2 us
    pallas_call x0 -> x1, Pallas kernels: none -> 29.8 us  [gather_x(): pl.pallas_call(lambda *refs: _gather_x_kernel(nx, *refs), out_shape=jax.S...]
    all_gather x1, waiting for transfers between devices: 40.9 us -> 25.2 us  [local(): w_rows = lax.all_gather(gather_x(w_out, nx), 'sz', axis=0, tiled=False)]
    pallas_call x1, Pallas kernels: 40.2 us -> 44.7 us  [gather_seq(): pl.pallas_call(lambda *refs: _gather_kernel(nx, nz, *refs), out_shape=jax...]
    unnamed x10 -> x12, local copies, waits for them, and re-layouts: 1.35 us -> 5.34 us
    convert_element_type x0 -> x1, local copies, waits for them, and re-layouts: none -> 2.88 us  [local(): terms.astype(jnp.bfloat16)]
    pallas_call x0 -> x1, local copies, waits for them, and re-layouts: none -> 2.31 us  [gather_x(): pl.pallas_call(lambda *refs: _gather_x_kernel(nx, *refs), out_shape=jax.S...]
  transfers between devices with their start and end apart: 2 -> 2, of which waited for: 2 -> 2; matrix products, arithmetic and copies ran while one was open for 10% -> 8% of each run, Pallas kernels for 25% -> 24%
where the time goes in v7:
time: 186 us
  Pallas kernels  74.5 us (40%)
  waiting for transfers between devices  65.3 us (35%)
  local copies, waits for them, and re-layouts  20.2 us (11%)
  between operations  14.1 us (8%)
  matrix products  11.6 us (6%)
    pallas_call x1, Pallas kernels, gather_seq(): pl.pallas_call(lambda *refs: _gather_kernel(nx, nz, *refs), out_shape=jax...  44.7 us
    reduce_scatter x1, waiting for transfers between devices, local(): lax.psum_scatter(terms.astype(jnp.bfloat16), 'head', scatter_dimension=0,...  40.1 us
    pallas_call x1, Pallas kernels, gather_x(): pl.pallas_call(lambda *refs: _gather_x_kernel(nx, *refs), out_shape=jax.S...  29.8 us
    all_gather x1, waiting for transfers between devices, local(): w_rows = lax.all_gather(gather_x(w_out, nx), 'sz', axis=0, tiled=False)  25.2 us
    optimization_barrier x1, local copies, waits for them, and re-layouts, local(): lax.optimization_barrier((every_change, cached_probs))  8.71 us
    dot_general x1, matrix products, local(): jnp.einsum('tk,hlxkc->xhtlc', attn_new, w_split, preferred_element_type=j...  7.29 us
    unnamed x12, local copies, waits for them, and re-layouts  5.34 us
    dot_general x1, matrix products, local(): jnp.einsum('qvgkij,qkjvd->qivgd', tiles, picked, preferred_element_type=j...  4.26 us
  transfers between devices with their start and end apart: 2, of which 2 were waited for; matrix products, arithmetic and copies ran while one was open for 8% of the time, Pallas kernels for 24%

profile of v7, /device:TPU:2, one launch (start us, length us, event | category | flops | bytes accessed | tf_op | source)
XLA Modules:
  0.0 186.0 jit_solution(6162948520404350342)
XLA Ops:
  7.2 0.0 all-gather.3.cloned.1.call-start
  7.2 1.8 copy.23.refs_0_
  9.0 29.8 %shard_map.78 = bf16[4,640,160]{2,1,0:T(8,128)(2,1)} custom-call(bf16[640,160]{1,0:T(8,128)(2,1)} %copy.23.refs_0_), custom_call_target="tpu_custom_call" | custom-call | tf_op jit(solution)/shard_map/pallas_call | solution.py:84
  38.8 2.3 %copy.24 = bf16[4,640,160]{1,2,0:T(8,128)(2,1)} copy(bf16[4,640,160]{2,1,0:T(8,128)(2,1)} %shard_map.78) | data formatting | bytes 1638400 | tf_op jit(solution)/shard_map/pallas_call | solution.py:84
  41.1 0.0 all-gather.3.cloned.1.call-update
  41.2 0.0 reduce-scatter.2.cloned.1.call-start
  41.2 44.7 %shard_map.77 = bf16[32,128,128]{2,1,0:T(8,128)(2,1)} custom-call(bf16[128,128]{1,0:T(8,128)(2,1)} %refs_0_.2), custom_call_target="tpu_custom_call" | custom-call | tf_op jit(solution)/shard_map/pallas_call | solution.py:100
  85.9 0.0 copy-start.2
  85.9 0.0 copy-start
  85.9 0.0 copy-start.3
  86.0 8.7 %copy.21 = bf16[4,5,8,128,128]{3,2,4,1,0:T(8,128)(2,1)} copy(bf16[4,5,8,128,128]{4,3,2,1,0:T(8,128)(2,1)} %param.6) | data formatting | bytes 10485760 | tf_op jit(solution)/shard_map/optimization_barrier | solution.py:123
  94.7 0.0 copy-done.2
  94.7 0.0 copy-start.1
  94.7 0.1 eq.15
  94.7 0.0 copy-done
  94.7 0.0 copy-done.3
  94.8 4.3 %convolution_bitcast_fusion = f32[4,128,1,5,128]{1,4,3,0,2:T(8,128)S(1)} fusion(bf16[4,5,8,128,128]{3,2,4,1,0:T(8,128)(2,1)} %copy.21, bf16[4,8,128,128]{3,2,1,0:T(8,128)(2,1)S(1)} %bitcast.40, s32[32]{0:T(128)S(1)} %copy-done.3, s32[32]{0:T(128)S(1)} %eq.15), kind=kOutput, calls=%fused_computation.2 | convolution fusion | flops 705168384 | bytes 7602432 | tf_op jit(solution)/shard_map/qvgkij,qkjvd->qivgd/dot_general | solution.py:130
  99.0 0.8 copy.22
  99.9 0.0 copy-done.1
  99.9 0.3 copy.20
  100.1 0.3 fusion.1
  100.4 25.2 %all-gather.3.cloned.1.call-done = bf16[32,640,160]{1,2,0:T(8,128)(2,1)} async-done(((bf16[4,640,160]{1,2,0:T(8,128)(2,1)}), bf16[32,640,160]{1,2,0:T(8,128)(2,1)}) %all-gather.3.cloned.1.call-update) | async-done | bytes 6553616 | tf_op jit(solution)/shard_map/all_gather | solution.py:121
  125.6 7.3 %convert_bitcast_fusion = bf16[4,2,512,4,160]{2,4,0,3,1:T(8,128)(2,1)S(1)} fusion(bf16[2,4,4,640,160]{3,4,2,1,0:T(8,128)(2,1)} %bitcast.42, bf16[512,640]{0,1:T(8,128)(2,1)S(1)} %fusion.1), kind=kOutput, calls=%fused_computation.1 | convolution fusion | flops 3358064640 | bytes 12451840 | tf_op jit(solution)/shard_map/tk,hlxkc->xhtlc/dot_general | solution.py:137
  132.9 2.9 %copy.26 = bf16[4,2,512,4,160]{2,4,3,1,0:T(8,128)(2,1)} copy(bf16[4,2,512,4,160]{2,4,0,3,1:T(8,128)(2,1)S(1)} %convert_bitcast_fusion) | data formatting | bytes 10485760 | tf_op jit(solution)/shard_map/convert_element_type | solution.py:139
  135.8 0.0 reduce-scatter.2.cloned.1.call-update
  135.8 1.1 copy.27
  136.9 40.1 %reduce-scatter.2.cloned.1.call-done = bf16[1,512,640]{1,2,0:T(8,128)(2,1)} async-done(((bf16[8,512,640]{1,2,0:T(8,128)(2,1)}), bf16[1,512,640]{1,2,0:T(8,128)(2,1)}) %reduce-scatter.2.cloned.1.call-update) | async-done | bytes 655376 | tf_op jit(solution)/shard_map/reduce_scatter | solution.py:139
  177.0 2.2 %copy.28 = bf16[512,640]{1,0:T(8,128)(2,1)} copy(bf16[512,640]{0,1:T(8,128)(2,1)} %bitcast.41) | data formatting | bytes 1310720
Async XLA Ops:
  7.2 118.4 %all-gather.3.cloned.1.call-start = ((), (), s32[]{:S(2)}) async-start(), calls=%async_computation.2 | async-start | bytes 7372800 | tf_op jit(solution)/shard_map/all_gather | solution.py:121
  41.2 135.8 %reduce-scatter.2.cloned.1.call-start = ((), (), s32[]{:S(2)}) async-start(), calls=%async_computation.1 | async-start | bytes 5898240 | tf_op jit(solution)/shard_map/reduce_scatter | solution.py:139
  85.9 8.7 %copy-start.2 = (s32[4,8]{1,0:T(4,128)S(1)}, s32[4,8]{1,0:T(4,128)}, u32[]{:S(2)}) copy-start(s32[4,8]{1,0:T(4,128)} %param.8) | copy-start | bytes 388
  85.9 8.8 %copy-start = (bf16[32,128,128]{2,1,0:T(8,128)(2,1)S(1)}, bf16[32,128,128]{2,1,0:T(8,128)(2,1)}, u32[]{:S(2)}) copy-start(bf16[32,128,128]{2,1,0:T(8,128)(2,1)} %shard_map.77) | copy-start | bytes 3145732
  85.9 8.8 %copy-start.3 = (s32[32]{0:T(128)S(1)}, s32[32]{0:T(128)}, u32[]{:S(2)}) copy-start(s32[32]{0:T(128)} %param.9) | copy-start | bytes 388
  94.7 5.2 %copy-start.1 = (bf16[512,640]{1,0:T(8,128)(2,1)S(1)}, bf16[512,640]{1,0:T(8,128)(2,1)}, u32[]{:S(2)}) copy-start(bf16[512,640]{1,0:T(8,128)(2,1)} %param.7) | copy-start | bytes 1966084
Sparse Core Ops, SparseCore 0:
  41.3 84.2 all-gather.2
  135.9 41.0 reduce-scatter.1

commit v8 on v6

--- a/solution.py
+++ b/solution.py
@@ -3,7 +3,7 @@
 from jax import lax
 from jax.experimental import pallas as pl
 from jax.experimental.pallas import tpu as pltpu
-from jax.sharding import PartitionSpec as P
+from jax.sharding import Mesh, PartitionSpec as P
 
 HD = 128
 BLK = 128
@@ -12,7 +12,8 @@
 
 def _gather_kernel(nx, nz, x_ref, o_ref, send1, recv1, send2, recv2, local_sem):
     me = lax.axis_index("seq")
-    hh = lax.axis_index("head")
+    hy = lax.axis_index("hy")
+    hc = lax.axis_index("hc")
     mx = me // nz
     mz = lax.rem(me, nz)
     own = pltpu.make_async_copy(x_ref, o_ref.at[me], local_sem)
@@ -25,7 +26,7 @@
             dst_ref=o_ref.at[me],
             send_sem=send1.at[k],
             recv_sem=recv1.at[k],
-            device_id=(peer, hh),
+            device_id=(peer, hy, hc),
             device_id_type=pl.DeviceIdType.MESH,
         )
         copy.start()
@@ -42,7 +43,7 @@
             dst_ref=o_ref.at[row],
             send_sem=send2.at[k],
             recv_sem=recv2.at[k],
-            device_id=(peer, hh),
+            device_id=(peer, hy, hc),
             device_id_type=pl.DeviceIdType.MESH,
         )
         copy.start()
@@ -91,27 +92,37 @@
     delta_out = delta_out.reshape(blocks_here * BLK, heads_here * HD)
     attn_new = (out_old.astype(jnp.float32) + delta_out).astype(jnp.bfloat16)
     n_head = w_full.shape[1] // attn_new.shape[1]
-    w_groups = w_full.reshape(w_full.shape[0], n_head, attn_new.shape[1])
-    terms = jnp.einsum("tk,kgc->gtc", attn_new, w_groups, preferred_element_type=jnp.float32)
-    out_proj = lax.psum_scatter(terms.astype(jnp.bfloat16), "head", scatter_dimension=0, tiled=True)[0]
+    width = attn_new.shape[1]
+    w_pairs = w_full.reshape(w_full.shape[0], n_head // 2, 2, width)
+    core = lax.axis_index("hc")
+    theirs = jnp.einsum("tk,kpc->ptc", attn_new, lax.dynamic_index_in_dim(w_pairs, 1 - core, axis=2, keepdims=False),
+                        preferred_element_type=jnp.float32).astype(jnp.bfloat16)
+    arrived = lax.ppermute(theirs, "hc", [(0, 1), (1, 0)])
+    mine = jnp.einsum("tk,kpc->ptc", attn_new, lax.dynamic_index_in_dim(w_pairs, core, axis=2, keepdims=False),
+                      preferred_element_type=jnp.float32).astype(jnp.bfloat16)
+    mine = lax.optimization_barrier(mine)
+    pair_sum = (mine.astype(jnp.float32) + arrived.astype(jnp.float32)).astype(jnp.bfloat16)
+    out_proj = lax.psum_scatter(pair_sum, "hy", scatter_dimension=0, tiled=True)[0]
     return (attn_new, out_proj)
 
 
 def solution(mesh):
+    head = ("hy", "hc")
     placed = (
-        P("seq", "head", None, None, None),
-        P("seq", "head"),
+        P("seq", head, None, None, None),
+        P("seq", head),
         P("seq", None),
         P(),
-        P("seq", "head"),
-        P("head", "seq"),
+        P("seq", head),
+        P(head, "seq"),
     )
     n_seq = mesh.shape["seq"]
     nz = 8 if n_seq % 8 == 0 else n_seq
+    split = Mesh(mesh.devices.reshape(n_seq, mesh.shape["head"] // 2, 2), ("seq", "hy", "hc"))
     return jax.shard_map(
         lambda *a: local(n_seq // nz, nz, *a),
-        mesh=mesh,
+        mesh=split,
         in_specs=placed,
-        out_specs=(P("seq", "head"), P("seq", "head")),
+        out_specs=(P("seq", head), P("seq", head)),
         check_vma=False,
     )

time: 161 us -> 164 us (1.019)
  waiting for transfers between devices: 81.5 us -> 76.6 us
  other arithmetic: 0.25 us -> 4.28 us
  local copies, waits for them, and re-layouts: 11 us -> 13.2 us
    reduce_scatter x1, waiting for transfers between devices: 40 us -> 34 us  [local(): lax.psum_scatter(pair_sum, 'hy', scatter_dimension=0, tiled=True)[0]]
    convert_element_type x0 -> x1, other arithmetic: none -> 4.03 us  [local(): (mine.astype(jnp.float32) + arrived.astype(jnp.float32)).astype(jnp.bfloa...]
    unnamed x10 -> x11, local copies, waits for them, and re-layouts: 1.35 us -> 3.51 us
    dot_general x1 -> x2, matrix products: 8.94 us -> 9.72 us  [the longest x1 5.6 us: local(): jnp.einsum('tk,kpc->ptc', attn_new, lax.dynamic_index_in_dim(w_pairs, 1 -...]
  transfers between devices with their start and end apart: 2 -> 3, of which waited for: 2 -> 3; matrix products, arithmetic and copies ran while one was open for 10% -> 12% of each run, Pallas kernels for 25% -> 25%
where the time goes in v8:
time: 164 us; the launch traced here: 162 us
  waiting for transfers between devices  76.6 us (47%)
  Pallas kernels  40.2 us (25%)
  between operations  14.1 us (9%)
  matrix products  13.9 us (8%)
  local copies, waits for them, and re-layouts  13.2 us (8%)
  other arithmetic  4.28 us (3%)
    all_gather x1, waiting for transfers between devices, local(): w_full = lax.all_gather(w_out, 'seq', axis=1, tiled=True)  40.8 us
    pallas_call x1, Pallas kernels, gather_seq(): pl.pallas_call(lambda *refs: _gather_kernel(nx, nz, *refs), out_shape=jax...  40.2 us
    reduce_scatter x1, waiting for transfers between devices, local(): lax.psum_scatter(pair_sum, 'hy', scatter_dimension=0, tiled=True)[0]  34 us
    optimization_barrier x1, local copies, waits for them, and re-layouts, local(): lax.optimization_barrier((every_change, cached_probs))  8.74 us
    dot_general x1, matrix products, local(): jnp.einsum('tk,kpc->ptc', attn_new, lax.dynamic_index_in_dim(w_pairs, 1 -...  5.6 us
    dot_general x1, matrix products, local(): jnp.einsum('qvgkij,qkjvd->qivgd', tiles, picked, preferred_element_type=j...  4.21 us
    dot_general x1, matrix products, local(): jnp.einsum('tk,kpc->ptc', attn_new, lax.dynamic_index_in_dim(w_pairs, cor...  4.12 us
    convert_element_type x1, other arithmetic, local(): (mine.astype(jnp.float32) + arrived.astype(jnp.float32)).astype(jnp.bfloa...  4.03 us
  transfers between devices with their start and end apart: 3, of which 3 were waited for; matrix products, arithmetic and copies ran while one was open for 12% of the time, Pallas kernels for 25%

profile of v8, /device:TPU:2, one launch (start us, length us, event | category | flops | bytes accessed | tf_op | source)
XLA Modules:
  0.0 162.5 jit_solution(13568525359114800314)
XLA Ops:
  7.2 0.0 all-gather.2.cloned.1.call-start
  7.2 0.7 all-gather.2.cloned.1.call-update
  7.9 0.0 reduce-scatter.2.cloned.1.call-start
  7.9 40.2 %shard_map.77 = bf16[32,128,128]{2,1,0:T(8,128)(2,1)} custom-call(bf16[128,128]{1,0:T(8,128)(2,1)} %refs_0_.1), custom_call_target="tpu_custom_call" | custom-call | tf_op jit(solution)/shard_map/pallas_call | solution.py:61
  48.2 0.0 copy-start.2
  48.2 0.0 copy-start
  48.2 0.0 copy-start.3
  48.2 8.7 %copy.22 = bf16[4,5,8,128,128]{3,2,4,1,0:T(8,128)(2,1)} copy(bf16[4,5,8,128,128]{4,3,2,1,0:T(8,128)(2,1)} %param.6) | data formatting | bytes 10485760 | tf_op jit(solution)/shard_map/optimization_barrier | solution.py:84
  57.0 0.0 copy-done.2
  57.0 0.1 eq.15
  57.1 0.0 copy-done
  57.1 0.0 copy-done.3
  57.1 0.0 copy-start.1
  57.1 4.2 %convolution_bitcast_fusion = f32[4,128,1,5,128]{1,4,3,0,2:T(8,128)S(1)} fusion(bf16[4,5,8,128,128]{3,2,4,1,0:T(8,128)(2,1)} %copy.22, bf16[4,8,128,128]{3,2,1,0:T(8,128)(2,1)S(1)} %bitcast.56, s32[32]{0:T(128)S(1)} %copy-done.3, s32[32]{0:T(128)S(1)} %eq.15), kind=kOutput, calls=%fused_computation.10 | convolution fusion | flops 705168384 | bytes 7602432 | tf_op jit(solution)/shard_map/qvgkij,qkjvd->qivgd/dot_general | solution.py:91
  61.3 0.8 copy.14
  62.1 0.0 copy-done.1
  62.1 0.3 copy.12
  62.4 0.3 fusion.11
  62.7 40.8 %all-gather.2.cloned.1.call-done = bf16[640,5120]{0,1:T(8,128)(2,1)} async-done(((bf16[640,160]{0,1:T(8,128)(2,1)}), bf16[640,5120]{0,1:T(8,128)(2,1)}) %all-gather.2.cloned.1.call-update) | async-done | bytes 6553616 | tf_op jit(solution)/shard_map/all_gather | solution.py:82
  103.5 5.6 %convert_bitcast_fusion = bf16[4,512,640]{1,2,0:T(8,128)(2,1)} fusion(bf16[640,4,2,640]{0,3,2,1:T(8,128)(2,1)} %bitcast.58, s32[]{:T(128)S(6)} %select_n.8, bf16[512,640]{0,1:T(8,128)(2,1)S(1)} %fusion.11), kind=kOutput, calls=%fused_computation.8 | convolution fusion | flops 1679032320 | bytes 6553604 | tf_op jit(solution)/shard_map/tk,kpc->ptc/dot_general | solution.py:98
  109.1 0.0 collective-permute-start
  109.1 4.1 %convert_bitcast_fusion.1 = bf16[4,512,640]{1,2,0:T(8,128)(2,1)S(1)} fusion(bf16[640,4,2,640]{0,3,2,1:T(8,128)(2,1)} %bitcast.59, s32[]{:T(128)S(6)} %select_n.7, bf16[512,640]{0,1:T(8,128)(2,1)S(1)} %fusion.11), kind=kOutput, calls=%fused_computation.9 | convolution fusion | flops 1679032320 | bytes 6553604 | tf_op jit(solution)/shard_map/tk,kpc->ptc/dot_general | solution.py:101
  113.2 1.1 collective-permute-done
  114.3 4.0 %add_convert_fusion = bf16[4,512,640]{1,2,0:T(8,128)(2,1)} fusion(bf16[4,512,640]{1,2,0:T(8,128)(2,1)} %collective-permute-done, bf16[4,512,640]{1,2,0:T(8,128)(2,1)S(1)} %convert_bitcast_fusion.1), kind=kLoop, calls=%fused_computation.1 | loop fusion | flops 5242880 | bytes 7864320 | tf_op jit(solution)/shard_map/convert_element_type | solution.py:104
  118.3 0.0 reduce-scatter.2.cloned.1.call-update
  118.4 1.1 copy.19
  119.4 34.0 %reduce-scatter.2.cloned.1.call-done = bf16[1,512,640]{1,2,0:T(8,128)(2,1)} async-done(((bf16[4,512,640]{1,2,0:T(8,128)(2,1)}), bf16[1,512,640]{1,2,0:T(8,128)(2,1)}) %reduce-scatter.2.cloned.1.call-update) | async-done | bytes 655376 | tf_op jit(solution)/shard_map/reduce_scatter | solution.py:105
  153.5 2.2 %copy.20 = bf16[512,640]{1,0:T(8,128)(2,1)} copy(bf16[512,640]{0,1:T(8,128)(2,1)} %bitcast.57) | data formatting | bytes 1310720
Async XLA Ops:
  7.2 96.3 %all-gather.2.cloned.1.call-start = ((), (), s32[]{:S(2)}) async-start(), calls=%async_computation.1 | async-start | bytes 6758400 | tf_op jit(solution)/shard_map/all_gather | solution.py:82
  7.9 145.6 %reduce-scatter.2.cloned.1.call-start = ((), (), s32[]{:S(2)}) async-start(), calls=%async_computation.2 | async-start | bytes 3276800 | tf_op jit(solution)/shard_map/reduce_scatter | solution.py:105
  48.2 8.8 %copy-start.2 = (s32[4,8]{1,0:T(4,128)S(1)}, s32[4,8]{1,0:T(4,128)}, u32[]{:S(2)}) copy-start(s32[4,8]{1,0:T(4,128)} %param.8) | copy-start | bytes 388
  48.2 8.8 %copy-start = (bf16[32,128,128]{2,1,0:T(8,128)(2,1)S(1)}, bf16[32,128,128]{2,1,0:T(8,128)(2,1)}, u32[]{:S(2)}) copy-start(bf16[32,128,128]{2,1,0:T(8,128)(2,1)} %shard_map.77) | copy-start | bytes 3145732
  48.2 8.8 %copy-start.3 = (s32[32]{0:T(128)S(1)}, s32[32]{0:T(128)}, u32[]{:S(2)}) copy-start(s32[32]{0:T(128)} %param.9) | copy-start | bytes 388
  57.1 5.1 %copy-start.1 = (bf16[512,640]{1,0:T(8,128)(2,1)S(1)}, bf16[512,640]{1,0:T(8,128)(2,1)}, u32[]{:S(2)}) copy-start(bf16[512,640]{1,0:T(8,128)(2,1)} %param.7) | copy-start | bytes 1966084
  109.1 5.3 %collective-permute-start = (bf16[4,512,640]{1,2,0:T(8,128)(2,1)}, bf16[4,512,640]{1,2,0:T(8,128)(2,1)}, u32[]{:S(2)}, u32[]{:S(2)}) collective-permute-start(bf16[4,512,640]{1,2,0:T(8,128)(2,1)} %convert_bitcast_fusion), channel_id=1, source_target_pairs={{0,1},{1,0},{2,3},{3,2},{4,5},{5,4},{6,7},{7,6},{8,9},{9,8},{10,11... | collective-permute-start | bytes 7864328 | tf_op jit(solution)/shard_map/ppermute | solution.py:100
Sparse Core Ops, SparseCore 0:
  10.6 92.8 all-gather.1
  118.5 34.9 reduce-scatter.1

commit v9 on v8

--- a/solution.py
+++ b/solution.py
@@ -95,13 +95,20 @@
     width = attn_new.shape[1]
     w_pairs = w_full.reshape(w_full.shape[0], n_head // 2, 2, width)
     core = lax.axis_index("hc")
-    theirs = jnp.einsum("tk,kpc->ptc", attn_new, lax.dynamic_index_in_dim(w_pairs, 1 - core, axis=2, keepdims=False),
-                        preferred_element_type=jnp.float32).astype(jnp.bfloat16)
-    arrived = lax.ppermute(theirs, "hc", [(0, 1), (1, 0)])
-    mine = jnp.einsum("tk,kpc->ptc", attn_new, lax.dynamic_index_in_dim(w_pairs, core, axis=2, keepdims=False),
-                      preferred_element_type=jnp.float32).astype(jnp.bfloat16)
-    mine = lax.optimization_barrier(mine)
-    pair_sum = (mine.astype(jnp.float32) + arrived.astype(jnp.float32)).astype(jnp.bfloat16)
+    theirs_w = lax.dynamic_index_in_dim(w_pairs, 1 - core, axis=2, keepdims=False)
+    mine_w = lax.dynamic_index_in_dim(w_pairs, core, axis=2, keepdims=False)
+    chunk = n_head // 4
+    sums = []
+    arrivals = []
+    for part in range(2):
+        cols = theirs_w[:, part * chunk:(part + 1) * chunk]
+        theirs = jnp.einsum("tk,kpc->ptc", attn_new, cols, preferred_element_type=jnp.float32).astype(jnp.bfloat16)
+        arrivals.append(lax.ppermute(theirs, "hc", [(0, 1), (1, 0)]))
+    for part in range(2):
+        cols = mine_w[:, part * chunk:(part + 1) * chunk]
+        mine = jnp.einsum("tk,kpc->ptc", attn_new, cols, preferred_element_type=jnp.float32).astype(jnp.bfloat16)
+        sums.append((mine.astype(jnp.float32) + arrivals[part].astype(jnp.float32)).astype(jnp.bfloat16))
+    pair_sum = jnp.concatenate(sums, axis=0)
     out_proj = lax.psum_scatter(pair_sum, "hy", scatter_dimension=0, tiled=True)[0]
     return (attn_new, out_proj)
 

time: 164 us -> 163 us (level)
  other arithmetic: 4.28 us -> 2 us
    convert_element_type x1 -> x0, other arithmetic: 4.03 us -> none  [local(): (mine.astype(jnp.float32) + arrived.astype(jnp.float32)).astype(jnp.bfloa...]
    concatenate x0 -> x1, other arithmetic: none -> 1.75 us  [local(): pair_sum = jnp.concatenate(sums, axis=0)]
    dot_general x2 -> x4, matrix products: 9.72 us -> 11.4 us  [local(): jnp.einsum('tk,kpc->ptc', attn_new, cols, preferred_element_type=jnp.floa...]
    unnamed x11 -> x13, local copies, waits for them, and re-layouts: 3.51 us -> 4.22 us
  transfers between devices with their start and end apart: 3 -> 4, of which waited for: 3 -> 3; matrix products, arithmetic and copies ran while one was open for 12% -> 13% of each run, Pallas kernels for 25% -> 25%
where the time goes in v9:
time: 163 us; the launch traced here: 162 us
  waiting for transfers between devices  75.5 us (46%)
  Pallas kernels  40.2 us (25%)
  matrix products  15.5 us (10%)
  between operations  14.1 us (9%)
  local copies, waits for them, and re-layouts  13.9 us (9%)
  other arithmetic  2 us (1%)
    all_gather x1, waiting for transfers between devices, local(): w_full = lax.all_gather(w_out, 'seq', axis=1, tiled=True)  40.7 us
    pallas_call x1, Pallas kernels, gather_seq(): pl.pallas_call(lambda *refs: _gather_kernel(nx, nz, *refs), out_shape=jax...  40.2 us
    reduce_scatter x1, waiting for transfers between devices, local(): lax.psum_scatter(pair_sum, 'hy', scatter_dimension=0, tiled=True)[0]  34 us
    dot_general x4, matrix products, local(): jnp.einsum('tk,kpc->ptc', attn_new, cols, preferred_element_type=jnp.floa...  11.4 us
    optimization_barrier x1, local copies, waits for them, and re-layouts, local(): lax.optimization_barrier((every_change, cached_probs))  8.72 us
    unnamed x13, local copies, waits for them, and re-layouts  4.22 us
    dot_general x1, matrix products, local(): jnp.einsum('qvgkij,qkjvd->qivgd', tiles, picked, preferred_element_type=j...  4.14 us
  transfers between devices with their start and end apart: 4, of which 3 were waited for; matrix products, arithmetic and copies ran while one was open for 13% of the time, Pallas kernels for 25%

profile of v9, /device:TPU:2, one launch (start us, length us, event | category | flops | bytes accessed | tf_op | source)
XLA Modules:
  0.0 161.8 jit_solution(17833777247280686430)
XLA Ops:
  7.2 0.0 all-gather.2.cloned.1.call-start
  7.2 0.7 all-gather.2.cloned.1.call-update
  7.9 0.0 reduce-scatter.2.cloned.1.call-start
  7.9 40.2 %shard_map.77 = bf16[32,128,128]{2,1,0:T(8,128)(2,1)} custom-call(bf16[128,128]{1,0:T(8,128)(2,1)} %refs_0_.1), custom_call_target="tpu_custom_call" | custom-call | tf_op jit(solution)/shard_map/pallas_call | solution.py:61
  48.2 0.0 copy-start.3
  48.2 0.0 copy-start.1
  48.2 0.0 copy-start.4
  48.2 8.7 %copy.24 = bf16[4,5,8,128,128]{3,2,4,1,0:T(8,128)(2,1)} copy(bf16[4,5,8,128,128]{4,3,2,1,0:T(8,128)(2,1)} %param.6) | data formatting | bytes 10485760 | tf_op jit(solution)/shard_map/optimization_barrier | solution.py:84
  57.0 0.0 copy-done.3
  57.0 0.1 eq.15
  57.0 0.0 copy-done.4
  57.0 4.1 %convolution_bitcast_fusion = f32[4,128,1,5,128]{1,4,3,0,2:T(8,128)S(1)} fusion(bf16[4,5,8,128,128]{3,2,4,1,0:T(8,128)(2,1)} %copy.24, bf16[4,8,128,128]{3,2,1,0:T(8,128)(2,1)S(1)} %bitcast.90, s32[32]{0:T(128)S(1)} %copy-done.4, s32[32]{0:T(128)S(1)} %eq.15), kind=kOutput, calls=%fused_computation.22 | convolution fusion | flops 705168384 | bytes 7602432 | tf_op jit(solution)/shard_map/qvgkij,qkjvd->qivgd/dot_general | solution.py:91
  61.2 0.0 copy-start.2
  61.2 0.8 copy.14
  62.1 0.2 copy-done.2
  62.3 0.2 copy.12
  62.5 0.3 fusion.37
  62.8 40.7 %all-gather.2.cloned.1.call-done = bf16[640,5120]{0,1:T(8,128)(2,1)} async-done(((bf16[640,160]{0,1:T(8,128)(2,1)}), bf16[640,5120]{0,1:T(8,128)(2,1)}) %all-gather.2.cloned.1.call-update) | async-done | bytes 6553616 | tf_op jit(solution)/shard_map/all_gather | solution.py:82
  103.5 3.7 %fusion.29 = bf16[2,512,640]{1,2,0:T(8,128)(2,1)} fusion(bf16[640,4,2,640]{0,3,2,1:T(8,128)(2,1)} %bitcast.85, s32[]{:T(128)S(6)} %select_n.8, bf16[512,640]{0,1:T(8,128)(2,1)S(1)} %fusion.37), kind=kOutput, calls=%fused_computation.24 | convolution fusion | flops 839516160 | bytes 5242884 | tf_op jit(solution)/shard_map/tk,kpc->ptc/dot_general | solution.py:105
  107.2 0.0 collective-permute-start
  107.2 3.7 %fusion.26 = bf16[2,512,640]{1,2,0:T(8,128)(2,1)} fusion(bf16[640,4,2,640]{0,3,2,1:T(8,128)(2,1)} %bitcast.86, s32[]{:T(128)S(6)} %select_n.8, bf16[512,640]{0,1:T(8,128)(2,1)S(1)} %fusion.37), kind=kOutput, calls=%fused_computation.23 | convolution fusion | flops 839516160 | bytes 5242884 | tf_op jit(solution)/shard_map/tk,kpc->ptc/dot_general | solution.py:105
  110.9 0.5 collective-permute-start.1
  111.4 0.0 collective-permute-done
  111.4 2.8 %fusion.13 = bf16[2,512,640]{1,2,0:T(8,128)(2,1)S(1)} fusion(bf16[2,512,640]{1,2,0:T(8,128)(2,1)S(1)} %collective-permute-done, bf16[640,4,2,640]{0,3,2,1:T(8,128)(2,1)} %bitcast.87, s32[]{:T(128)S(6)} %select_n.7, bf16[512,640]{0,1:T(8,128)(2,1)S(1)} %fusion.37), kind=kOutput, calls=%fused_computation.17 | convolution fusion | flops 842137600 | bytes 6553604 | tf_op jit(solution)/shard_map/tk,kpc->ptc/dot_general | solution.py:109
  114.1 0.1 collective-permute-done.1
  114.2 0.5 copy-done
  114.7 1.2 fusion.12
  115.9 1.8 %pad_maximum_fusion = bf16[4,512,640]{1,2,0:T(8,128)(2,1)} fusion(bf16[2,512,640]{1,2,0:T(8,128)(2,1)S(1)} %fusion.12, bf16[2,512,640]{1,2,0:T(8,128)(2,1)S(1)} %fusion.13), kind=kLoop, calls=%fused_computation.13 | loop fusion | flops 1310720 | bytes 5242880 | tf_op jit(solution)/shard_map/concatenate | solution.py:111
  117.7 0.0 reduce-scatter.2.cloned.1.call-update
  117.7 1.1 copy.21
  118.8 34.0 %reduce-scatter.2.cloned.1.call-done = bf16[1,512,640]{1,2,0:T(8,128)(2,1)} async-done(((bf16[4,512,640]{1,2,0:T(8,128)(2,1)}), bf16[1,512,640]{1,2,0:T(8,128)(2,1)}) %reduce-scatter.2.cloned.1.call-update) | async-done | bytes 655376 | tf_op jit(solution)/shard_map/reduce_scatter | solution.py:112
  152.8 2.2 %copy.22 = bf16[512,640]{1,0:T(8,128)(2,1)} copy(bf16[512,640]{0,1:T(8,128)(2,1)} %bitcast.91) | data formatting | bytes 1310720
  (2 shorter events, 0.0 us)
Async XLA Ops:
  7.2 96.3 %all-gather.2.cloned.1.call-start = ((), (), s32[]{:S(2)}) async-start(), calls=%async_computation.1 | async-start | bytes 6758400 | tf_op jit(solution)/shard_map/all_gather | solution.py:82
  7.9 144.9 %reduce-scatter.2.cloned.1.call-start = ((), (), s32[]{:S(2)}) async-start(), calls=%async_computation.2 | async-start | bytes 3276800 | tf_op jit(solution)/shard_map/reduce_scatter | solution.py:112
  48.2 8.8 %copy-start.3 = (s32[4,8]{1,0:T(4,128)S(1)}, s32[4,8]{1,0:T(4,128)}, u32[]{:S(2)}) copy-start(s32[4,8]{1,0:T(4,128)} %param.8) | copy-start | bytes 388
  48.2 8.8 %copy-start.1 = (bf16[32,128,128]{2,1,0:T(8,128)(2,1)S(1)}, bf16[32,128,128]{2,1,0:T(8,128)(2,1)}, u32[]{:S(2)}) copy-start(bf16[32,128,128]{2,1,0:T(8,128)(2,1)} %shard_map.77) | copy-start | bytes 3145732
  48.2 8.8 %copy-start.4 = (s32[32]{0:T(128)S(1)}, s32[32]{0:T(128)}, u32[]{:S(2)}) copy-start(s32[32]{0:T(128)} %param.9) | copy-start | bytes 388
  61.2 1.1 copy-start.2
  107.2 4.2 %collective-permute-start = (bf16[2,512,640]{1,2,0:T(8,128)(2,1)}, bf16[2,512,640]{1,2,0:T(8,128)(2,1)S(1)}, u32[]{:S(2)}, u32[]{:S(2)}) collective-permute-start(bf16[2,512,640]{1,2,0:T(8,128)(2,1)} %fusion.29), channel_id=1, source_target_pairs={{0,1},{1,0},{2,3},{3,2},{4,5},{5,4},{6,7},{7,6},{8,9},{9,8},{10,11... | collective-permute-start | bytes 3932168 | tf_op jit(solution)/shard_map/ppermute | solution.py:106
  110.9 3.4 %collective-permute-start.1 = (bf16[2,512,640]{1,2,0:T(8,128)(2,1)}, bf16[2,512,640]{1,2,0:T(8,128)(2,1)S(1)}, u32[]{:S(2)}, u32[]{:S(2)}) collective-permute-start(bf16[2,512,640]{1,2,0:T(8,128)(2,1)} %fusion.26), channel_id=1, source_target_pairs={{0,1},{1,0},{2,3},{3,2},{4,5},{5,4},{6,7},{7,6},{8,9},{9,8},{10,11... | collective-permute-start | bytes 3932168 | tf_op jit(solution)/shard_map/ppermute | solution.py:106
  111.4 3.4 %copy-start = (bf16[640,5120]{0,1:T(8,128)(2,1)S(1)}, bf16[640,5120]{0,1:T(8,128)(2,1)}, u32[]{:S(2)}) copy-start(bf16[640,5120]{0,1:T(8,128)(2,1)} %all-gather.2.cloned.1.call-done) | copy-start | bytes 19660804
Sparse Core Ops, SparseCore 0:
  10.6 92.8 all-gather.1
  117.8 34.9 reduce-scatter.1

commit v10 on v5

--- a/solution.py
+++ b/solution.py
@@ -73,29 +73,28 @@
     )(x)
 
 
-def _project_kernel(a_ref, w_ref, o_ref):
-    term = lax.dot_general(a_ref[...], w_ref[...], (((1,), (1,)), ((), ())), preferred_element_type=jnp.float32)
-    o_ref[0] = term.astype(o_ref.dtype)
+def _project_kernel(w_ref, a_ref, o_ref):
+    o_ref[0] = jnp.dot(w_ref[...], a_ref[...], preferred_element_type=jnp.float32).astype(o_ref.dtype)
 
 
-def project(a, w_t):
-    rows, width = a.shape
+def project_t(w_t, a_t):
+    width, rows = a_t.shape
     groups = w_t.shape[0] // width
     return pl.pallas_call(
         _project_kernel,
-        out_shape=jax.ShapeDtypeStruct((groups, rows, width), a.dtype),
+        out_shape=jax.ShapeDtypeStruct((groups, width, rows), a_t.dtype),
         grid=(groups,),
         in_specs=[
-            pl.BlockSpec((rows, width), lambda g: (0, 0)),
             pl.BlockSpec((width, w_t.shape[1]), lambda g: (g, 0)),
+            pl.BlockSpec((width, rows), lambda g: (0, 0)),
         ],
-        out_specs=pl.BlockSpec((1, rows, width), lambda g: (g, 0, 0)),
+        out_specs=pl.BlockSpec((1, width, rows), lambda g: (g, 0, 0)),
         cost_estimate=pl.CostEstimate(
             flops=2 * rows * width * w_t.shape[0],
-            bytes_accessed=2 * (a.size + w_t.size + groups * rows * width),
+            bytes_accessed=2 * (a_t.size + w_t.size + groups * rows * width),
             transcendentals=0,
         ),
-    )(a, w_t)
+    )(w_t, a_t)
 
 
 def local(nx, nz, cached_probs, out_old, key_lists, changed_block_numbers, delta_v, w_out):
@@ -105,6 +104,7 @@
     values_here = heads_here // GROUP
     w_full = lax.all_gather(w_out, "seq", axis=1, tiled=True)
     every_change = gather_seq(delta_v, nx, nz)
+    every_change, cached_probs = lax.optimization_barrier((every_change, cached_probs))
     every_change = every_change.reshape(nx * nz * delta_v.shape[0] // BLK, BLK * values_here * HD)
     flat_lists = key_lists.reshape(blocks_here * topk_here)
     onehot = (flat_lists[:, None] == changed_block_numbers[None, :]).astype(jnp.bfloat16)
@@ -114,8 +114,8 @@
     delta_out = jnp.einsum("qvgkij,qkjvd->qivgd", tiles, picked, preferred_element_type=jnp.float32)
     delta_out = delta_out.reshape(blocks_here * BLK, heads_here * HD)
     attn_new = (out_old.astype(jnp.float32) + delta_out).astype(jnp.bfloat16)
-    terms = project(attn_new, w_full.T)
-    out_proj = lax.psum_scatter(terms.astype(jnp.bfloat16), "head", scatter_dimension=0, tiled=True)[0]
+    terms_t = project_t(w_full.T, attn_new.T)
+    out_proj = lax.psum_scatter(terms_t, "head", scatter_dimension=0, tiled=True)[0].T
     return (attn_new, out_proj)
 
 

time: 165 us -> 164 us (level)
  local copies, waits for them, and re-layouts: 9.64 us -> 14.5 us
  waiting for transfers between devices: 82.9 us -> 79.4 us
    optimization_barrier x0 -> x1, local copies, waits for them, and re-layouts: none -> 8.74 us  [local(): lax.optimization_barrier((every_change, cached_probs))]
    unnamed x5 -> x13, local copies, waits for them, and re-layouts: 8.65 us -> 4.8 us
    reduce_scatter x1, waiting for transfers between devices: 41 us -> 38.9 us  [local(): lax.psum_scatter(terms_t, 'head', scatter_dimension=0, tiled=True)[0]]
where the time goes in v10:
time: 164 us; the launch traced here: 163 us
  waiting for transfers between devices  79.4 us (48%)
  Pallas kernels  50.2 us (31%)
  local copies, waits for them, and re-layouts  14.5 us (9%)
  between operations  14.1 us (9%)
  matrix products  4.14 us (3%)
    pallas_call x1, Pallas kernels, gather_seq(): pl.pallas_call(lambda *refs: _gather_kernel(nx, nz, *refs), out_shape=jax...  40.2 us
    all_gather x1, waiting for transfers between devices, local(): w_full = lax.all_gather(w_out, 'seq', axis=1, tiled=True)  39.8 us
    reduce_scatter x1, waiting for transfers between devices, local(): lax.psum_scatter(terms_t, 'head', scatter_dimension=0, tiled=True)[0]  38.9 us
    pallas_call x1, Pallas kernels, project_t(): pl.pallas_call(_project_kernel, out_shape=jax.ShapeDtypeStruct((groups, w...  9.91 us
    optimization_barrier x1, local copies, waits for them, and re-layouts, local(): lax.optimization_barrier((every_change, cached_probs))  8.74 us
    unnamed x13, local copies, waits for them, and re-layouts  4.8 us
    dot_general x1, matrix products, local(): jnp.einsum('qvgkij,qkjvd->qivgd', tiles, picked, preferred_element_type=j...  4.14 us
  transfers between devices with their start and end apart: 2, of which 2 were waited for; matrix products, arithmetic and copies ran while one was open for 10% of the time, Pallas kernels for 25%

profile of v10, /device:TPU:2, one launch (start us, length us, event | category | flops | bytes accessed | tf_op | source)
XLA Modules:
  0.0 163.5 jit_solution(17562863762781084998)
XLA Ops:
  7.2 0.0 all-gather.2.cloned.1.call-start
  7.2 0.7 all-gather.2.cloned.1.call-update
  7.9 0.0 reduce-scatter.2.cloned.1.call-start
  7.9 40.2 %shard_map.77 = bf16[32,128,128]{2,1,0:T(8,128)(2,1)} custom-call(bf16[128,128]{1,0:T(8,128)(2,1)} %refs_0_.1), custom_call_target="tpu_custom_call" | custom-call | tf_op jit(solution)/shard_map/pallas_call | solution.py:60
  48.2 0.0 copy-start.3
  48.2 0.0 copy-start.1
  48.2 0.0 copy-start.4
  48.2 8.7 %copy.14 = bf16[4,5,8,128,128]{3,2,4,1,0:T(8,128)(2,1)} copy(bf16[4,5,8,128,128]{4,3,2,1,0:T(8,128)(2,1)} %param.6) | data formatting | bytes 10485760 | tf_op jit(solution)/shard_map/optimization_barrier | solution.py:107
  57.0 0.0 copy-done.3
  57.0 0.1 eq.15
  57.1 0.0 copy-done.1
  57.1 0.0 copy-done.4
  57.1 4.1 %convolution_bitcast_fusion = f32[4,128,1,5,128]{1,4,3,0,2:T(8,128)S(1)} fusion(bf16[4,5,8,128,128]{3,2,4,1,0:T(8,128)(2,1)} %copy.14, bf16[4,8,128,128]{3,2,1,0:T(8,128)(2,1)S(1)} %bitcast.37, s32[32]{0:T(128)S(1)} %copy-done.4, s32[32]{0:T(128)S(1)} %eq.15), kind=kOutput, calls=%fused_computation.1 | convolution fusion | flops 705168384 | bytes 7602432 | tf_op jit(solution)/shard_map/qvgkij,qkjvd->qivgd/dot_general | solution.py:114
  61.2 0.0 copy-start.2
  61.2 0.8 copy.10
  62.1 0.2 copy-done.2
  62.3 0.2 copy.8
  62.6 1.1 fusion.1
  63.6 39.8 %all-gather.2.cloned.1.call-done = bf16[640,5120]{0,1:T(8,128)(2,1)} async-done(((bf16[640,160]{0,1:T(8,128)(2,1)}), bf16[640,5120]{0,1:T(8,128)(2,1)}) %all-gather.2.cloned.1.call-update) | async-done | bytes 6553616 | tf_op jit(solution)/shard_map/all_gather | solution.py:105
  103.5 9.9 %shard_map.78 = bf16[8,640,512]{2,1,0:T(8,128)(2,1)} custom-call(bf16[5120,640]{1,0:T(8,128)(2,1)} %bitcast.34, bf16[640,512]{1,0:T(8,128)(2,1)} %bitcast.35), custom_call_target="tpu_custom_call" | custom-call | flops 3355443200 | bytes 12451840 | tf_op jit(solution)/shard_map/pallas_call | solution.py:83
  113.4 0.0 copy-start
  113.4 0.0 reduce-scatter.2.cloned.1.call-update
  113.4 1.1 copy-done
  114.5 1.1 copy.11
  115.6 38.9 %reduce-scatter.2.cloned.1.call-done = bf16[1,640,512]{2,1,0:T(8,128)(2,1)} async-done(((bf16[8,640,512]{2,1,0:T(8,128)(2,1)}), bf16[1,640,512]{2,1,0:T(8,128)(2,1)}) %reduce-scatter.2.cloned.1.call-update) | async-done | bytes 655376 | tf_op jit(solution)/shard_map/reduce_scatter | solution.py:118
  154.5 2.2 %copy.12 = bf16[512,640]{1,0:T(8,128)(2,1)} copy(bf16[512,640]{0,1:T(8,128)(2,1)} %bitcast.38) | data formatting | bytes 1310720
Async XLA Ops:
  7.2 96.3 %all-gather.2.cloned.1.call-start = ((), (), s32[]{:S(2)}) async-start(), calls=%async_computation.1 | async-start | bytes 6758400 | tf_op jit(solution)/shard_map/all_gather | solution.py:105
  7.9 146.6 %reduce-scatter.2.cloned.1.call-start = ((), (), s32[]{:S(2)}) async-start(), calls=%async_computation.2 | async-start | bytes 5898240 | tf_op jit(solution)/shard_map/reduce_scatter | solution.py:118
  48.2 8.8 %copy-start.3 = (s32[4,8]{1,0:T(4,128)S(1)}, s32[4,8]{1,0:T(4,128)}, u32[]{:S(2)}) copy-start(s32[4,8]{1,0:T(4,128)} %param.8) | copy-start | bytes 388
  48.2 8.8 %copy-start.1 = (bf16[32,128,128]{2,1,0:T(8,128)(2,1)S(1)}, bf16[32,128,128]{2,1,0:T(8,128)(2,1)}, u32[]{:S(2)}) copy-start(bf16[32,128,128]{2,1,0:T(8,128)(2,1)} %shard_map.77) | copy-start | bytes 3145732
  48.2 8.8 %copy-start.4 = (s32[32]{0:T(128)S(1)}, s32[32]{0:T(128)}, u32[]{:S(2)}) copy-start(s32[32]{0:T(128)} %param.9) | copy-start | bytes 388
  61.2 1.1 copy-start.2
  113.4 1.1 copy-start
Sparse Core Ops, SparseCore 0:
  10.6 92.8 all-gather.1
  113.5 40.8 reduce-scatter.1

commit v11 on v6

--- a/solution.py
+++ b/solution.py
@@ -73,6 +73,33 @@
     )(x)
 
 
+def _refresh_kernel(p_ref, v_ref, o_ref, out_ref):
+    acc = o_ref[...].astype(jnp.float32)
+    for k in range(p_ref.shape[2]):
+        acc += jnp.dot(p_ref[0, 0, k], v_ref[0, k], preferred_element_type=jnp.float32)
+    out_ref[...] = acc.astype(out_ref.dtype)
+
+
+def refresh(cached_probs, picked, out_old):
+    blocks, heads, topk = cached_probs.shape[:3]
+    return pl.pallas_call(
+        _refresh_kernel,
+        out_shape=jax.ShapeDtypeStruct(out_old.shape, out_old.dtype),
+        grid=(blocks, heads),
+        in_specs=[
+            pl.BlockSpec((1, 1, topk, BLK, BLK), lambda q, h: (q, h, 0, 0, 0)),
+            pl.BlockSpec((1, topk, BLK, HD), lambda q, h: (q, 0, 0, h // GROUP)),
+            pl.BlockSpec((BLK, HD), lambda q, h: (q, h)),
+        ],
+        out_specs=pl.BlockSpec((BLK, HD), lambda q, h: (q, h)),
+        cost_estimate=pl.CostEstimate(
+            flops=2 * blocks * heads * topk * BLK * BLK * HD,
+            bytes_accessed=2 * (cached_probs.size + picked.size + 2 * out_old.size),
+            transcendentals=0,
+        ),
+    )(cached_probs, picked, out_old)
+
+
 def local(nx, nz, cached_probs, out_old, key_lists, changed_block_numbers, delta_v, w_out):
     blocks_here = cached_probs.shape[0]
     heads_here = cached_probs.shape[1]
@@ -85,11 +112,8 @@
     flat_lists = key_lists.reshape(blocks_here * topk_here)
     onehot = (flat_lists[:, None] == changed_block_numbers[None, :]).astype(jnp.bfloat16)
     selected = jnp.dot(onehot, every_change, preferred_element_type=jnp.float32)
-    picked = selected.astype(jnp.bfloat16).reshape(blocks_here, topk_here, BLK, values_here, HD)
-    tiles = cached_probs.reshape(blocks_here, values_here, GROUP, topk_here, BLK, BLK)
-    delta_out = jnp.einsum("qvgkij,qkjvd->qivgd", tiles, picked, preferred_element_type=jnp.float32)
-    delta_out = delta_out.reshape(blocks_here * BLK, heads_here * HD)
-    attn_new = (out_old.astype(jnp.float32) + delta_out).astype(jnp.bfloat16)
+    picked = selected.astype(jnp.bfloat16).reshape(blocks_here, topk_here, BLK, values_here * HD)
+    attn_new = refresh(cached_probs, picked, out_old)
     n_head = w_full.shape[1] // attn_new.shape[1]
     w_groups = w_full.reshape(w_full.shape[0], n_head, attn_new.shape[1])
     terms = jnp.einsum("tk,kgc->gtc", attn_new, w_groups, preferred_element_type=jnp.float32)

time: 161 us -> 160 us (level)
  Pallas kernels: 40.2 us -> 53.6 us
  local copies, waits for them, and re-layouts: 11 us -> 1.98 us
  waiting for transfers between devices: 81.5 us -> 78.5 us
    pallas_call x0 -> x1, Pallas kernels: none -> 13.8 us  [refresh(): pl.pallas_call(_refresh_kernel, out_shape=jax.ShapeDtypeStruct(out_old.sh...]
    optimization_barrier x1 -> x0, local copies, waits for them, and re-layouts: 8.72 us -> none  [local(): lax.optimization_barrier((every_change, cached_probs))]
    all_gather x1, waiting for transfers between devices: 40.9 us -> 36.8 us  [local(): w_full = lax.all_gather(w_out, 'seq', axis=1, tiled=True)]
    dot_general x1, matrix products: 4.19 us -> 1.98 us  [local(): selected = jnp.dot(onehot, every_change, preferred_element_type=jnp.float32)]
  transfers between devices with their start and end apart: 2 -> 2, of which waited for: 2 -> 2; matrix products, arithmetic and copies ran while one was open for 10% -> 2% of each run, Pallas kernels for 25% -> 34%
where the time goes in v11:
time: 160 us
  waiting for transfers between devices  78.5 us (49%)
  Pallas kernels  53.6 us (34%)
  between operations  14.1 us (9%)
  matrix products  11.7 us (7%)
  local copies, waits for them, and re-layouts  1.98 us (1%)
    reduce_scatter x1, waiting for transfers between devices, local(): lax.psum_scatter(terms.astype(jnp.bfloat16), 'head', scatter_dimension=0,...  41 us
    pallas_call x1, Pallas kernels, gather_seq(): pl.pallas_call(lambda *refs: _gather_kernel(nx, nz, *refs), out_shape=jax...  39.8 us
    all_gather x1, waiting for transfers between devices, local(): w_full = lax.all_gather(w_out, 'seq', axis=1, tiled=True)  36.8 us
    pallas_call x1, Pallas kernels, refresh(): pl.pallas_call(_refresh_kernel, out_shape=jax.ShapeDtypeStruct(out_old.sh...  13.8 us
    dot_general x1, matrix products, local(): jnp.einsum('tk,kgc->gtc', attn_new, w_groups, preferred_element_type=jnp....  9.73 us
  transfers between devices with their start and end apart: 2, of which 2 were waited for; matrix products, arithmetic and copies ran while one was open for 2% of the time, Pallas kernels for 34%

profile of v11, /device:TPU:2, one launch (start us, length us, event | category | flops | bytes accessed | tf_op | source)
XLA Modules:
  0.0 160.0 jit_solution(10337832977370677953)
XLA Ops:
  7.2 0.0 all-gather.2.cloned.1.call-start
  7.2 0.7 all-gather.2.cloned.1.call-update
  7.9 0.0 reduce-scatter.2.cloned.1.call-start
  7.9 0.8 eq.15
  8.7 39.8 %shard_map.77 = bf16[32,128,128]{2,1,0:T(8,128)(2,1)} custom-call(bf16[128,128]{1,0:T(8,128)(2,1)} %refs_0_.1), custom_call_target="tpu_custom_call" | custom-call | tf_op jit(solution)/shard_map/pallas_call | solution.py:60
  48.5 2.0 %fusion = bf16[4,8,128,128]{3,1,2,0:T(8,128)(2,1)S(1)} fusion(bf16[4,8,128,128]{3,2,1,0:T(8,128)(2,1)} %bitcast.18, s32[32]{0:T(128)} %param.9, s32[32]{0:T(128)S(1)} %eq.15), kind=kOutput, calls=%fused_computation.2 | convolution fusion | flops 34079744 | bytes 2097408 | tf_op jit(solution)/shard_map/dot_general | solution.py:114
  50.5 1.2 copy.17
  51.8 13.8 %shard_map.78 = bf16[512,640]{1,0:T(8,128)(2,1)} custom-call(bf16[4,5,8,128,128]{4,3,2,1,0:T(8,128)(2,1)} %p_ref, bf16[4,8,128,128]{3,2,1,0:T(8,128)(2,1)} %copy.17, bf16[512,640]{1,0:T(8,128)(2,1)} %o_ref.1), custom_call_target="tpu_custom_call" | custom-call | flops 671088640 | bytes 7602176 | tf_op jit(solution)/shard_map/pallas_call | solution.py:85
  65.5 36.8 %all-gather.2.cloned.1.call-done = bf16[640,5120]{0,1:T(8,128)(2,1)} async-done(((bf16[640,160]{0,1:T(8,128)(2,1)}), bf16[640,5120]{0,1:T(8,128)(2,1)}) %all-gather.2.cloned.1.call-update) | async-done | bytes 6553616 | tf_op jit(solution)/shard_map/all_gather | solution.py:108
  102.3 9.7 %convert_bitcast_fusion = bf16[8,512,640]{2,1,0:T(8,128)(2,1)} fusion(bf16[640,8,640]{0,2,1:T(8,128)(2,1)} %bitcast.19, bf16[512,640]{1,0:T(8,128)(2,1)} %shard_map.78), kind=kOutput, calls=%fused_computation.1 | convolution fusion | flops 3358064640 | bytes 12451840 | tf_op jit(solution)/shard_map/tk,kgc->gtc/dot_general | solution.py:119
  112.1 0.0 reduce-scatter.2.cloned.1.call-update
  112.1 41.0 %reduce-scatter.2.cloned.1.call-done = bf16[1,512,640]{2,1,0:T(8,128)(2,1)} async-done(((bf16[8,512,640]{2,1,0:T(8,128)(2,1)}), bf16[1,512,640]{2,1,0:T(8,128)(2,1)}) %reduce-scatter.2.cloned.1.call-update) | async-done | bytes 655376 | tf_op jit(solution)/shard_map/reduce_scatter | solution.py:120
Async XLA Ops:
  7.2 95.2 %all-gather.2.cloned.1.call-start = ((), (), s32[]{:S(2)}) async-start(), calls=%async_computation.1 | async-start | bytes 6758400 | tf_op jit(solution)/shard_map/all_gather | solution.py:108
  7.9 145.2 %reduce-scatter.2.cloned.1.call-start = ((), (), s32[]{:S(2)}) async-start(), calls=%async_computation.2 | async-start | bytes 5898240 | tf_op jit(solution)/shard_map/reduce_scatter | solution.py:120
Sparse Core Ops, SparseCore 0:
  10.6 91.7 all-gather.1
  112.2 40.8 reduce-scatter.1

commit v12 on v11

--- a/solution.py
+++ b/solution.py
@@ -73,25 +73,33 @@
     )(x)
 
 
-def _refresh_kernel(p_ref, v_ref, o_ref, out_ref):
+def _refresh_kernel(p_ref, v_ref, o_ref, out_ref, cols_ref):
     acc = o_ref[...].astype(jnp.float32)
     for k in range(p_ref.shape[2]):
         acc += jnp.dot(p_ref[0, 0, k], v_ref[0, k], preferred_element_type=jnp.float32)
-    out_ref[...] = acc.astype(out_ref.dtype)
+    result = acc.astype(out_ref.dtype)
+    out_ref[...] = result
+    cols_ref[...] = result.T
 
 
 def refresh(cached_probs, picked, out_old):
     blocks, heads, topk = cached_probs.shape[:3]
     return pl.pallas_call(
         _refresh_kernel,
-        out_shape=jax.ShapeDtypeStruct(out_old.shape, out_old.dtype),
+        out_shape=(
+            jax.ShapeDtypeStruct(out_old.shape, out_old.dtype),
+            jax.ShapeDtypeStruct(out_old.shape[::-1], out_old.dtype),
+        ),
         grid=(blocks, heads),
         in_specs=[
             pl.BlockSpec((1, 1, topk, BLK, BLK), lambda q, h: (q, h, 0, 0, 0)),
             pl.BlockSpec((1, topk, BLK, HD), lambda q, h: (q, 0, 0, h // GROUP)),
             pl.BlockSpec((BLK, HD), lambda q, h: (q, h)),
         ],
-        out_specs=pl.BlockSpec((BLK, HD), lambda q, h: (q, h)),
+        out_specs=(
+            pl.BlockSpec((BLK, HD), lambda q, h: (q, h)),
+            pl.BlockSpec((HD, BLK), lambda q, h: (h, q)),
+        ),
         cost_estimate=pl.CostEstimate(
             flops=2 * blocks * heads * topk * BLK * BLK * HD,
             bytes_accessed=2 * (cached_probs.size + picked.size + 2 * out_old.size),
@@ -113,10 +121,10 @@
     onehot = (flat_lists[:, None] == changed_block_numbers[None, :]).astype(jnp.bfloat16)
     selected = jnp.dot(onehot, every_change, preferred_element_type=jnp.float32)
     picked = selected.astype(jnp.bfloat16).reshape(blocks_here, topk_here, BLK, values_here * HD)
-    attn_new = refresh(cached_probs, picked, out_old)
+    attn_new, attn_cols = refresh(cached_probs, picked, out_old)
     n_head = w_full.shape[1] // attn_new.shape[1]
     w_groups = w_full.reshape(w_full.shape[0], n_head, attn_new.shape[1])
-    terms = jnp.einsum("tk,kgc->gtc", attn_new, w_groups, preferred_element_type=jnp.float32)
+    terms = jnp.einsum("kt,kgc->gtc", attn_cols, w_groups, preferred_element_type=jnp.float32)
     out_proj = lax.psum_scatter(terms.astype(jnp.bfloat16), "head", scatter_dimension=0, tiled=True)[0]
     return (attn_new, out_proj)
 

time: 160 us -> 162 us (1.012)
  no operation moved by 1% of the time
where the time goes in v12:
time: 162 us; the launch traced here: 161 us
  waiting for transfers between devices  78.9 us (49%)
  Pallas kernels  54.5 us (34%)
  between operations  14.1 us (9%)
  matrix products  11.7 us (7%)
  local copies, waits for them, and re-layouts  1.98 us (1%)
    reduce_scatter x1, waiting for transfers between devices, local(): lax.psum_scatter(terms.astype(jnp.bfloat16), 'head', scatter_dimension=0,...  41 us
    pallas_call x1, Pallas kernels, gather_seq(): pl.pallas_call(lambda *refs: _gather_kernel(nx, nz, *refs), out_shape=jax...  40.2 us
    all_gather x1, waiting for transfers between devices, local(): w_full = lax.all_gather(w_out, 'seq', axis=1, tiled=True)  37.1 us
    pallas_call x1, Pallas kernels, refresh(): pl.pallas_call(_refresh_kernel, out_shape=(jax.ShapeDtypeStruct(out_old.s...  14.2 us
    dot_general x1, matrix products, local(): jnp.einsum('kt,kgc->gtc', attn_cols, w_groups, preferred_element_type=jnp...  9.74 us
  transfers between devices with their start and end apart: 2, of which 2 were waited for; matrix products, arithmetic and copies ran while one was open for 2% of the time, Pallas kernels for 34%

profile of v12, /device:TPU:2, one launch (start us, length us, event | category | flops | bytes accessed | tf_op | source)
XLA Modules:
  0.0 161.2 jit_solution(16018338295010461327)
XLA Ops:
  7.2 0.0 all-gather.2.cloned.1.call-start
  7.2 0.7 all-gather.2.cloned.1.call-update
  7.9 0.0 reduce-scatter.2.cloned.1.call-start
  7.9 40.2 %shard_map.77 = bf16[32,128,128]{2,1,0:T(8,128)(2,1)} custom-call(bf16[128,128]{1,0:T(8,128)(2,1)} %refs_0_.1), custom_call_target="tpu_custom_call" | custom-call | tf_op jit(solution)/shard_map/pallas_call | solution.py:60
  48.2 0.8 eq.15
  49.0 2.0 %fusion = bf16[4,8,128,128]{3,1,2,0:T(8,128)(2,1)S(1)} fusion(bf16[4,8,128,128]{3,2,1,0:T(8,128)(2,1)} %bitcast.18, s32[32]{0:T(128)} %param.9, s32[32]{0:T(128)S(1)} %eq.15), kind=kOutput, calls=%fused_computation.2 | convolution fusion | flops 34079744 | bytes 2097408 | tf_op jit(solution)/shard_map/dot_general | solution.py:122
  51.0 1.2 copy.21
  52.2 14.2 %shard_map.78 = (bf16[512,640]{1,0:T(8,128)(2,1)}, bf16[640,512]{1,0:T(8,128)(2,1)}) custom-call(bf16[4,5,8,128,128]{4,3,2,1,0:T(8,128)(2,1)} %p_ref, bf16[4,8,128,128]{3,2,1,0:T(8,128)(2,1)} %copy.21, bf16[512,640]{1,0:T(8,128)(2,1)} %o_ref.1), custom_call_target="tpu_custom_call" | custom-call | flops 671088640 | bytes 7602176 | tf_op jit(solution)/shard_map/pallas_call | solution.py:87
  66.4 37.1 %all-gather.2.cloned.1.call-done = bf16[640,5120]{0,1:T(8,128)(2,1)} async-done(((bf16[640,160]{0,1:T(8,128)(2,1)}), bf16[640,5120]{0,1:T(8,128)(2,1)}) %all-gather.2.cloned.1.call-update) | async-done | bytes 6553616 | tf_op jit(solution)/shard_map/all_gather | solution.py:116
  103.5 9.7 %convert_bitcast_fusion = bf16[8,512,640]{2,1,0:T(8,128)(2,1)} fusion(bf16[640,8,640]{0,2,1:T(8,128)(2,1)} %bitcast.19, bf16[640,512]{1,0:T(8,128)(2,1)} %get-tuple-element.9), kind=kOutput, calls=%fused_computation.1 | convolution fusion | flops 3358064640 | bytes 12451840 | tf_op jit(solution)/shard_map/kt,kgc->gtc/dot_general | solution.py:127
  113.3 0.0 reduce-scatter.2.cloned.1.call-update
  113.3 41.0 %reduce-scatter.2.cloned.1.call-done = bf16[1,512,640]{2,1,0:T(8,128)(2,1)} async-done(((bf16[8,512,640]{2,1,0:T(8,128)(2,1)}), bf16[1,512,640]{2,1,0:T(8,128)(2,1)}) %reduce-scatter.2.cloned.1.call-update) | async-done | bytes 655376 | tf_op jit(solution)/shard_map/reduce_scatter | solution.py:128
Async XLA Ops:
  7.2 96.4 %all-gather.2.cloned.1.call-start = ((), (), s32[]{:S(2)}) async-start(), calls=%async_computation.1 | async-start | bytes 6758400 | tf_op jit(solution)/shard_map/all_gather | solution.py:116
  7.9 146.4 %reduce-scatter.2.cloned.1.call-start = ((), (), s32[]{:S(2)}) async-start(), calls=%async_computation.2 | async-start | bytes 5898240 | tf_op jit(solution)/shard_map/reduce_scatter | solution.py:128
Sparse Core Ops, SparseCore 0:
  10.6 92.9 all-gather.1
  113.4 40.8 reduce-scatter.1

commit v13 on v6

--- a/solution.py
+++ b/solution.py
@@ -78,7 +78,8 @@
     heads_here = cached_probs.shape[1]
     topk_here = cached_probs.shape[2]
     values_here = heads_here // GROUP
-    w_full = lax.all_gather(w_out, "seq", axis=1, tiled=True)
+    padded = jnp.pad(w_out, ((0, 8), (0, 0)))
+    w_full = lax.all_gather(padded, "seq", axis=1, tiled=True)[:w_out.shape[0]]
     every_change = gather_seq(delta_v, nx, nz)
     every_change, cached_probs = lax.optimization_barrier((every_change, cached_probs))
     every_change = every_change.reshape(nx * nz * delta_v.shape[0] // BLK, BLK * values_here * HD)

time: 161 us -> 169 us (1.050)
  local copies, waits for them, and re-layouts: 11 us -> 19.4 us
  matrix products: 13.1 us -> 10.1 us
  waiting for transfers between devices: 81.5 us -> 83.8 us
    unnamed x10 -> x7, local copies, waits for them, and re-layouts: 1.35 us -> 4.58 us
    dot_general x1, matrix products: 8.94 us -> 5.97 us  [local(): jnp.einsum('tk,kgc->gtc', attn_new, w_groups, preferred_element_type=jnp....]
    all_gather x1, waiting for transfers between devices: 40.9 us -> 43.8 us  [local(): w_full = lax.all_gather(padded, 'seq', axis=1, tiled=True)[:w_out.shape[0]]]
    slice x0 -> x2, local copies, waits for them, and re-layouts: none -> 2.86 us  [local(): w_full = lax.all_gather(padded, 'seq', axis=1, tiled=True)[:w_out.shape[0]]]
  transfers between devices with their start and end apart: 2 -> 2, of which waited for: 2 -> 2; matrix products, arithmetic and copies ran while one was open for 10% -> 10% of each run, Pallas kernels for 25% -> 24%
where the time goes in v13:
time: 169 us
  waiting for transfers between devices  83.8 us (50%)
  Pallas kernels  40.9 us (24%)
  local copies, waits for them, and re-layouts  19.4 us (11%)
  between operations  14.1 us (8%)
  matrix products  10.1 us (6%)
    all_gather x1, waiting for transfers between devices, local(): w_full = lax.all_gather(padded, 'seq', axis=1, tiled=True)[:w_out.shape[0]]  43.8 us
    pallas_call x1, Pallas kernels, gather_seq(): pl.pallas_call(lambda *refs: _gather_kernel(nx, nz, *refs), out_shape=jax...  40.9 us
    reduce_scatter x1, waiting for transfers between devices, local(): lax.psum_scatter(terms.astype(jnp.bfloat16), 'head', scatter_dimension=0,...  39.9 us
    optimization_barrier x1, local copies, waits for them, and re-layouts, local(): lax.optimization_barrier((every_change, cached_probs))  8.74 us
    dot_general x1, matrix products, local(): jnp.einsum('tk,kgc->gtc', attn_new, w_groups, preferred_element_type=jnp....  5.97 us
    unnamed x7, local copies, waits for them, and re-layouts  4.58 us
    dot_general x1, matrix products, local(): jnp.einsum('qvgkij,qkjvd->qivgd', tiles, picked, preferred_element_type=j...  4.15 us
  transfers between devices with their start and end apart: 2, of which 2 were waited for; matrix products, arithmetic and copies ran while one was open for 10% of the time, Pallas kernels for 24%

profile of v13, /device:TPU:2, one launch (start us, length us, event | category | flops | bytes accessed | tf_op | source)
XLA Modules:
  0.0 168.7 jit_solution(12163851032284866108)
XLA Ops:
  7.2 0.0 all-gather.2.cloned.1.call-start
  7.2 1.6 pad.4
  8.9 0.0 all-gather.2.cloned.1.call-update
  8.9 0.0 reduce-scatter.2.cloned.1.call-start
  8.9 0.8 eq.15
  9.7 1.3 copy.10
  11.0 40.9 %shard_map.77 = bf16[32,128,128]{2,1,0:T(8,128)(2,1)} custom-call(bf16[128,128]{1,0:T(8,128)(2,1)} %refs_0_.1), custom_call_target="tpu_custom_call" | custom-call | tf_op jit(solution)/shard_map/pallas_call | solution.py:60
  52.0 0.0 copy-start
  52.0 0.0 copy-start.1
  52.0 8.7 %copy.17 = bf16[4,5,8,128,128]{3,2,4,1,0:T(8,128)(2,1)} copy(bf16[4,5,8,128,128]{4,3,2,1,0:T(8,128)(2,1)} %param.6) | data formatting | bytes 10485760 | tf_op jit(solution)/shard_map/optimization_barrier | solution.py:84
  60.7 0.0 copy-done
  60.7 0.0 copy-done.1
  60.7 4.1 %convolution_bitcast_fusion = f32[4,128,1,5,128]{1,4,3,0,2:T(8,128)S(1)} fusion(bf16[4,5,8,128,128]{3,2,4,1,0:T(8,128)(2,1)} %copy.17, bf16[4,8,128,128]{3,2,1,0:T(8,128)(2,1)S(1)} %bitcast.39, s32[32]{0:T(128)S(1)} %copy-done.1, s32[32]{0:T(128)S(1)} %eq.15), kind=kOutput, calls=%fused_computation.2 | convolution fusion | flops 705168384 | bytes 7602432 | tf_op jit(solution)/shard_map/qvgkij,qkjvd->qivgd/dot_general | solution.py:91
  64.9 0.8 copy.12
  65.8 0.3 fusion.1
  66.0 43.8 %all-gather.2.cloned.1.call-done = bf16[648,5120]{0,1:T(8,128)(2,1)} async-done(((bf16[648,160]{0,1:T(8,128)(2,1)}), bf16[648,5120]{0,1:T(8,128)(2,1)}) %all-gather.2.cloned.1.call-update) | async-done | bytes 6635536 | tf_op jit(solution)/shard_map/all_gather | solution.py:82
  109.8 0.0 slice-start
  109.8 2.9 %slice-done = bf16[640,5120]{0,1:T(8,128)(2,1)S(1)} async-done(((bf16[648,5120]{0,1:T(8,128)(2,1)}), bf16[640,5120]{0,1:T(8,128)(2,1)S(1)}, s32[]{:S(2)}) %slice-start) | async-done | bytes 6553624 | tf_op jit(solution)/shard_map/slice | solution.py:82
  112.7 6.0 %convert_bitcast_fusion = bf16[8,512,640]{1,2,0:T(8,128)(2,1)} fusion(bf16[640,8,640]{0,2,1:T(8,128)(2,1)S(1)} %bitcast.37, bf16[512,640]{0,1:T(8,128)(2,1)S(1)} %fusion.1), kind=kOutput, calls=%fused_computation.1 | convolution fusion | flops 3358064640 | bytes 12451840 | tf_op jit(solution)/shard_map/tk,kgc->gtc/dot_general | solution.py:96
  118.6 0.0 reduce-scatter.2.cloned.1.call-update
  118.7 1.1 copy.14
  119.7 39.9 %reduce-scatter.2.cloned.1.call-done = bf16[1,512,640]{1,2,0:T(8,128)(2,1)} async-done(((bf16[8,512,640]{1,2,0:T(8,128)(2,1)}), bf16[1,512,640]{1,2,0:T(8,128)(2,1)}) %reduce-scatter.2.cloned.1.call-update) | async-done | bytes 655376 | tf_op jit(solution)/shard_map/reduce_scatter | solution.py:97
  159.7 2.2 %copy.15 = bf16[512,640]{1,0:T(8,128)(2,1)} copy(bf16[512,640]{0,1:T(8,128)(2,1)} %bitcast.40) | data formatting | bytes 1310720
Async XLA Ops:
  7.2 102.7 %all-gather.2.cloned.1.call-start = ((), (), s32[]{:S(2)}) async-start(), calls=%async_computation.1 | async-start | bytes 8110080 | tf_op jit(solution)/shard_map/all_gather | solution.py:82
  8.9 150.8 %reduce-scatter.2.cloned.1.call-start = ((), (), s32[]{:S(2)}) async-start(), calls=%async_computation.2 | async-start | bytes 5898240 | tf_op jit(solution)/shard_map/reduce_scatter | solution.py:97
  52.0 8.8 %copy-start = (bf16[32,128,128]{2,1,0:T(8,128)(2,1)S(1)}, bf16[32,128,128]{2,1,0:T(8,128)(2,1)}, u32[]{:S(2)}) copy-start(bf16[32,128,128]{2,1,0:T(8,128)(2,1)} %shard_map.77) | copy-start | bytes 3145732
  52.0 8.8 %copy-start.1 = (s32[32]{0:T(128)S(1)}, s32[32]{0:T(128)}, u32[]{:S(2)}) copy-start(s32[32]{0:T(128)} %param.9) | copy-start | bytes 388
  109.8 2.9 %slice-start = ((bf16[648,5120]{0,1:T(8,128)(2,1)}), bf16[640,5120]{0,1:T(8,128)(2,1)S(1)}, s32[]{:S(2)}) async-start(bf16[648,5120]{0,1:T(8,128)(2,1)} %all-gather.2.cloned.1.call-done), calls=%async_computation.3 | async-start | bytes 13107200 | tf_op jit(solution)/shard_map/slice | solution.py:82
Sparse Core Ops, SparseCore 0:
  11.2 98.6 all-gather.1
  118.8 40.8 reduce-scatter.1

commit v14 on v6

--- a/solution.py
+++ b/solution.py
@@ -92,8 +92,12 @@
     attn_new = (out_old.astype(jnp.float32) + delta_out).astype(jnp.bfloat16)
     n_head = w_full.shape[1] // attn_new.shape[1]
     w_groups = w_full.reshape(w_full.shape[0], n_head, attn_new.shape[1])
-    terms = jnp.einsum("tk,kgc->gtc", attn_new, w_groups, preferred_element_type=jnp.float32)
-    out_proj = lax.psum_scatter(terms.astype(jnp.bfloat16), "head", scatter_dimension=0, tiled=True)[0]
+    width = attn_new.shape[1]
+    terms = jnp.stack([
+        jnp.dot(attn_new, w_full[:, g * width:(g + 1) * width], preferred_element_type=jnp.float32).astype(jnp.bfloat16)
+        for g in range(n_head)
+    ])
+    out_proj = lax.psum_scatter(terms, "head", scatter_dimension=0, tiled=True)[0]
     return (attn_new, out_proj)
 
 

time: 161 us -> 169 us (1.050)
  matrix products: 13.1 us -> 21 us
    dot_general x1 -> x8, matrix products: 8.94 us -> 16.8 us  [local(): jnp.dot(attn_new, w_full[:, g * width:(g + 1) * width], preferred_element...]
  transfers between devices with their start and end apart: 2 -> 2, of which waited for: 2 -> 2; matrix products, arithmetic and copies ran while one was open for 10% -> 9% of each run, Pallas kernels for 25% -> 24%
where the time goes in v14:
time: 169 us; the launch traced here: 168 us
  waiting for transfers between devices  81.5 us (48%)
  Pallas kernels  40.2 us (24%)
  matrix products  21 us (12%)
  between operations  14.1 us (8%)
  local copies, waits for them, and re-layouts  11 us (7%)
    all_gather x1, waiting for transfers between devices, local(): w_full = lax.all_gather(w_out, 'seq', axis=1, tiled=True)  40.8 us
    pallas_call x1, Pallas kernels, gather_seq(): pl.pallas_call(lambda *refs: _gather_kernel(nx, nz, *refs), out_shape=jax...  40.2 us
    reduce_scatter x1, waiting for transfers between devices, local(): lax.psum_scatter(terms, 'head', scatter_dimension=0, tiled=True)[0]  40 us
    dot_general x8, matrix products, local(): jnp.dot(attn_new, w_full[:, g * width:(g + 1) * width], preferred_element...  16.8 us
    optimization_barrier x1, local copies, waits for them, and re-layouts, local(): lax.optimization_barrier((every_change, cached_probs))  8.74 us
    dot_general x1, matrix products, local(): jnp.einsum('qvgkij,qkjvd->qivgd', tiles, picked, preferred_element_type=j...  4.19 us
  transfers between devices with their start and end apart: 2, of which 2 were waited for; matrix products, arithmetic and copies ran while one was open for 9% of the time, Pallas kernels for 24%

profile of v14, /device:TPU:2, one launch (start us, length us, event | category | flops | bytes accessed | tf_op | source)
XLA Modules:
  0.0 168.2 jit_solution(5181862526984953056)
XLA Ops:
  7.2 0.0 all-gather.2.cloned.1.call-start
  7.2 0.7 all-gather.2.cloned.1.call-update
  7.9 0.0 reduce-scatter.2.cloned.1.call-start
  7.9 40.2 %shard_map.77 = bf16[32,128,128]{2,1,0:T(8,128)(2,1)} custom-call(bf16[128,128]{1,0:T(8,128)(2,1)} %refs_0_.1), custom_call_target="tpu_custom_call" | custom-call | tf_op jit(solution)/shard_map/pallas_call | solution.py:60
  48.2 0.0 copy-start.2
  48.2 0.0 copy-start
  48.2 0.0 copy-start.3
  48.2 8.7 %copy.14 = bf16[4,5,8,128,128]{3,2,4,1,0:T(8,128)(2,1)} copy(bf16[4,5,8,128,128]{4,3,2,1,0:T(8,128)(2,1)} %param.6) | data formatting | bytes 10485760 | tf_op jit(solution)/shard_map/optimization_barrier | solution.py:83
  57.0 0.0 copy-done.2
  57.0 0.0 copy-start.1
  57.0 0.1 eq.15
  57.1 0.0 copy-done
  57.1 0.0 copy-done.3
  57.1 4.2 %convolution_bitcast_fusion = f32[4,128,1,5,128]{1,4,3,0,2:T(8,128)S(1)} fusion(bf16[4,5,8,128,128]{3,2,4,1,0:T(8,128)(2,1)} %copy.14, bf16[4,8,128,128]{3,2,1,0:T(8,128)(2,1)S(1)} %bitcast.71, s32[32]{0:T(128)S(1)} %copy-done.3, s32[32]{0:T(128)S(1)} %eq.15), kind=kOutput, calls=%fused_computation.1 | convolution fusion | flops 705168384 | bytes 7602432 | tf_op jit(solution)/shard_map/qvgkij,qkjvd->qivgd/dot_general | solution.py:90
  61.3 0.8 copy.11
  62.1 0.0 copy-done.1
  62.1 0.3 copy.9
  62.4 0.3 fusion.1
  62.6 40.8 %all-gather.2.cloned.1.call-done = bf16[640,5120]{0,1:T(8,128)(2,1)} async-done(((bf16[640,160]{0,1:T(8,128)(2,1)}), bf16[640,5120]{0,1:T(8,128)(2,1)}) %all-gather.2.cloned.1.call-update) | async-done | bytes 6553616 | tf_op jit(solution)/shard_map/all_gather | solution.py:81
  103.5 0.0 copy-start.4
  103.5 2.9 %fusion.3 = bf16[8,512,640]{2,1,0:T(8,128)(2,1)} fusion(bf16[512,640]{0,1:T(8,128)(2,1)S(1)} %fusion.1, bf16[640,5120]{0,1:T(8,128)(2,1)} %all-gather.2.cloned.1.call-done), kind=kOutput, calls=%fused_computation.14 | convolution fusion | flops 419758080 | bytes 2129920 | tf_op jit(solution)/shard_map/dot_general | solution.py:97
  106.4 2.8 %fusion.5 = bf16[8,512,640]{2,1,0:T(8,128)(2,1)} fusion(bf16[8,512,640]{2,1,0:T(8,128)(2,1)} %fusion.3, bf16[512,640]{0,1:T(8,128)(2,1)S(1)} %fusion.1, bf16[640,5120]{0,1:T(8,128)(2,1)} %all-gather.2.cloned.1.call-done), kind=kOutput, calls=%fused_computation.16 | convolution fusion | flops 419758080 | bytes 2129920 | tf_op jit(solution)/shard_map/dot_general | solution.py:97
  109.2 2.9 %fusion.7 = bf16[8,512,640]{2,1,0:T(8,128)(2,1)} fusion(bf16[8,512,640]{2,1,0:T(8,128)(2,1)} %fusion.5, bf16[512,640]{0,1:T(8,128)(2,1)S(1)} %fusion.1, bf16[640,5120]{0,1:T(8,128)(2,1)} %all-gather.2.cloned.1.call-done), kind=kOutput, calls=%fused_computation.18 | convolution fusion | flops 419758080 | bytes 2129920 | tf_op jit(solution)/shard_map/dot_general | solution.py:97
  112.1 0.0 copy-done.4
  112.1 1.7 %fusion.9 = bf16[8,512,640]{2,1,0:T(8,128)(2,1)} fusion(bf16[8,512,640]{2,1,0:T(8,128)(2,1)} %fusion.7, bf16[512,640]{0,1:T(8,128)(2,1)S(1)} %fusion.1, bf16[640,5120]{0,1:T(8,128)(2,1)S(1)} %copy-done.4), kind=kOutput, calls=%fused_computation.20 | convolution fusion | flops 419758080 | bytes 2129920 | tf_op jit(solution)/shard_map/dot_general | solution.py:97
  113.8 1.6 fusion.11
  115.4 1.6 fusion.13
  117.0 1.6 fusion.15
  118.7 1.6 fusion.17
  120.3 0.0 reduce-scatter.2.cloned.1.call-update
  120.3 1.1 copy.12
  121.4 40.0 %reduce-scatter.2.cloned.1.call-done = bf16[1,512,640]{2,1,0:T(8,128)(2,1)} async-done(((bf16[8,512,640]{2,1,0:T(8,128)(2,1)}), bf16[1,512,640]{2,1,0:T(8,128)(2,1)}) %reduce-scatter.2.cloned.1.call-update) | async-done | bytes 655376 | tf_op jit(solution)/shard_map/reduce_scatter | solution.py:100
Async XLA Ops:
  7.2 96.3 %all-gather.2.cloned.1.call-start = ((), (), s32[]{:S(2)}) async-start(), calls=%async_computation.1 | async-start | bytes 6758400 | tf_op jit(solution)/shard_map/all_gather | solution.py:81
  7.9 153.5 %reduce-scatter.2.cloned.1.call-start = ((), (), s32[]{:S(2)}) async-start(), calls=%async_computation.2 | async-start | bytes 5898240 | tf_op jit(solution)/shard_map/reduce_scatter | solution.py:100
  48.2 8.8 %copy-start.2 = (s32[4,8]{1,0:T(4,128)S(1)}, s32[4,8]{1,0:T(4,128)}, u32[]{:S(2)}) copy-start(s32[4,8]{1,0:T(4,128)} %param.8) | copy-start | bytes 388
  48.2 8.8 %copy-start = (bf16[32,128,128]{2,1,0:T(8,128)(2,1)S(1)}, bf16[32,128,128]{2,1,0:T(8,128)(2,1)}, u32[]{:S(2)}) copy-start(bf16[32,128,128]{2,1,0:T(8,128)(2,1)} %shard_map.77) | copy-start | bytes 3145732
  48.2 8.8 %copy-start.3 = (s32[32]{0:T(128)S(1)}, s32[32]{0:T(128)}, u32[]{:S(2)}) copy-start(s32[32]{0:T(128)} %param.9) | copy-start | bytes 388
  57.0 5.1 %copy-start.1 = (bf16[512,640]{1,0:T(8,128)(2,1)S(1)}, bf16[512,640]{1,0:T(8,128)(2,1)}, u32[]{:S(2)}) copy-start(bf16[512,640]{1,0:T(8,128)(2,1)} %param.7) | copy-start | bytes 1966084
  103.5 8.6 %copy-start.4 = (bf16[640,5120]{0,1:T(8,128)(2,1)S(1)}, bf16[640,5120]{0,1:T(8,128)(2,1)}, u32[]{:S(2)}) copy-start(bf16[640,5120]{0,1:T(8,128)(2,1)} %all-gather.2.cloned.1.call-done) | copy-start | bytes 19660804
Sparse Core Ops, SparseCore 0:
  10.6 92.8 all-gather.1
  120.4 40.8 reduce-scatter.1

commit v15 on v5

--- a/solution.py
+++ b/solution.py
@@ -73,23 +73,45 @@
     )(x)
 
 
-def _project_kernel(a_ref, w_ref, o_ref):
-    term = lax.dot_general(a_ref[...], w_ref[...], (((1,), (1,)), ((), ())), preferred_element_type=jnp.float32)
+def _project_kernel(chunks, a_ref, w_hbm, o_ref, w_vmem, sems):
+    g = pl.program_id(0)
+    width = a_ref.shape[1]
+    rows = w_vmem.shape[0] // chunks
+    per_chunk = rows // width
+
+    def copy(i):
+        part = pl.ds(i * rows, rows)
+        return pltpu.make_async_copy(w_hbm.at[part], w_vmem.at[part], sems.at[i])
+
+    @pl.when(g == 0)
+    def _start():
+        for i in range(chunks):
+            copy(i).start()
+
+    for i in range(chunks):
+        pl.when(g == i * per_chunk)(lambda i=i: copy(i).wait())
+
+    w = w_vmem[pl.ds(pl.multiple_of(g * width, width), width), :]
+    term = lax.dot_general(a_ref[...], w, (((1,), (1,)), ((), ())), preferred_element_type=jnp.float32)
     o_ref[0] = term.astype(o_ref.dtype)
 
 
-def project(a, w_t):
+def project(a, w_t, chunks=4):
     rows, width = a.shape
     groups = w_t.shape[0] // width
     return pl.pallas_call(
-        _project_kernel,
+        lambda *refs: _project_kernel(chunks, *refs),
         out_shape=jax.ShapeDtypeStruct((groups, rows, width), a.dtype),
         grid=(groups,),
         in_specs=[
             pl.BlockSpec((rows, width), lambda g: (0, 0)),
-            pl.BlockSpec((width, w_t.shape[1]), lambda g: (g, 0)),
+            pl.BlockSpec(memory_space=pl.ANY),
         ],
         out_specs=pl.BlockSpec((1, rows, width), lambda g: (g, 0, 0)),
+        scratch_shapes=[
+            pltpu.VMEM(w_t.shape, w_t.dtype),
+            pltpu.SemaphoreType.DMA((chunks,)),
+        ],
         cost_estimate=pl.CostEstimate(
             flops=2 * rows * width * w_t.shape[0],
             bytes_accessed=2 * (a.size + w_t.size + groups * rows * width),
@@ -105,6 +127,7 @@
     values_here = heads_here // GROUP
     w_full = lax.all_gather(w_out, "seq", axis=1, tiled=True)
     every_change = gather_seq(delta_v, nx, nz)
+    every_change, cached_probs = lax.optimization_barrier((every_change, cached_probs))
     every_change = every_change.reshape(nx * nz * delta_v.shape[0] // BLK, BLK * values_here * HD)
     flat_lists = key_lists.reshape(blocks_here * topk_here)
     onehot = (flat_lists[:, None] == changed_block_numbers[None, :]).astype(jnp.bfloat16)
@@ -115,7 +138,7 @@
     delta_out = delta_out.reshape(blocks_here * BLK, heads_here * HD)
     attn_new = (out_old.astype(jnp.float32) + delta_out).astype(jnp.bfloat16)
     terms = project(attn_new, w_full.T)
-    out_proj = lax.psum_scatter(terms.astype(jnp.bfloat16), "head", scatter_dimension=0, tiled=True)[0]
+    out_proj = lax.psum_scatter(terms, "head", scatter_dimension=0, tiled=True)[0]
     return (attn_new, out_proj)
 
 

time: 165 us -> 162 us (0.982)
  waiting for transfers between devices: 82.9 us -> 80.9 us
    optimization_barrier x0 -> x1, local copies, waits for them, and re-layouts: none -> 8.74 us  [local(): lax.optimization_barrier((every_change, cached_probs))]
    unnamed x5 -> x6, local copies, waits for them, and re-layouts: 8.65 us -> 0.02 us
    all_gather x1, waiting for transfers between devices: 41.2 us -> 39.1 us  [local(): w_full = lax.all_gather(w_out, 'seq', axis=1, tiled=True)]
where the time goes in v15:
time: 162 us; the launch traced here: 161 us
  waiting for transfers between devices  80.9 us (50%)
  Pallas kernels  50.2 us (31%)
  between operations  14.1 us (9%)
  local copies, waits for them, and re-layouts  9.74 us (6%)
  matrix products  4.14 us (3%)
  other arithmetic  2.24 us (1%)
    reduce_scatter x1, waiting for transfers between devices, local(): lax.psum_scatter(terms, 'head', scatter_dimension=0, tiled=True)[0]  41.1 us
    pallas_call x1, Pallas kernels, gather_seq(): pl.pallas_call(lambda *refs: _gather_kernel(nx, nz, *refs), out_shape=jax...  40.2 us
    all_gather x1, waiting for transfers between devices, local(): w_full = lax.all_gather(w_out, 'seq', axis=1, tiled=True)  39.1 us
    pallas_call x1, Pallas kernels, project(): pl.pallas_call(lambda *refs: _project_kernel(chunks, *refs), out_shape=ja...  9.92 us
    optimization_barrier x1, local copies, waits for them, and re-layouts, local(): lax.optimization_barrier((every_change, cached_probs))  8.74 us
    dot_general x1, matrix products, local(): jnp.einsum('qvgkij,qkjvd->qivgd', tiles, picked, preferred_element_type=j...  4.14 us
  transfers between devices with their start and end apart: 2, of which 2 were waited for; matrix products, arithmetic and copies ran while one was open for 10% of the time, Pallas kernels for 25%

profile of v15, /device:TPU:2, one launch (start us, length us, event | category | flops | bytes accessed | tf_op | source)
XLA Modules:
  0.0 161.4 jit_solution(8665151661990942626)
XLA Ops:
  7.2 0.0 all-gather.2.cloned.1.call-start
  7.2 0.7 all-gather.2.cloned.1.call-update
  7.9 0.0 reduce-scatter.2.cloned.1.call-start
  7.9 40.2 %shard_map.77 = bf16[32,128,128]{2,1,0:T(8,128)(2,1)} custom-call(bf16[128,128]{1,0:T(8,128)(2,1)} %refs_0_.1), custom_call_target="tpu_custom_call" | custom-call | tf_op jit(solution)/shard_map/pallas_call | solution.py:60
  48.2 0.0 copy-start.1
  48.2 0.0 copy-start
  48.2 0.0 copy-start.2
  48.2 8.7 %copy.14 = bf16[4,5,8,128,128]{3,2,4,1,0:T(8,128)(2,1)} copy(bf16[4,5,8,128,128]{4,3,2,1,0:T(8,128)(2,1)} %param.6) | data formatting | bytes 10485760 | tf_op jit(solution)/shard_map/optimization_barrier | solution.py:130
  57.0 0.0 copy-done.1
  57.0 0.1 eq.15
  57.1 0.0 copy-done
  57.1 0.0 copy-done.2
  57.1 4.1 %convolution_bitcast_fusion = f32[4,128,1,5,128]{1,4,3,0,2:T(8,128)S(1)} fusion(bf16[4,5,8,128,128]{3,2,4,1,0:T(8,128)(2,1)} %copy.14, bf16[4,8,128,128]{3,2,1,0:T(8,128)(2,1)S(1)} %bitcast.32, s32[32]{0:T(128)S(1)} %copy-done.2, s32[32]{0:T(128)S(1)} %eq.15), kind=kOutput, calls=%fused_computation.1 | convolution fusion | flops 705168384 | bytes 7602432 | tf_op jit(solution)/shard_map/qvgkij,qkjvd->qivgd/dot_general | solution.py:137
  61.2 0.9 copy.18
  62.1 2.2 %fusion.1.refs_0_ = bf16[512,640]{1,0:T(8,128)(2,1)} fusion(f32[64,8,5,128]{3,2,1,0:T(8,128)S(1)} %bitcast.30, bf16[512,640]{1,0:T(8,128)(2,1)} %param.7), kind=kLoop, calls=%fused_computation.4 | loop fusion | flops 983040 | bytes 2621440 | tf_op jit(solution)/shard_map/convert_element_type | solution.py:139
  64.4 39.1 %all-gather.2.cloned.1.call-done = bf16[640,5120]{0,1:T(8,128)(2,1)} async-done(((bf16[640,160]{0,1:T(8,128)(2,1)}), bf16[640,5120]{0,1:T(8,128)(2,1)}) %all-gather.2.cloned.1.call-update) | async-done | bytes 6553616 | tf_op jit(solution)/shard_map/all_gather | solution.py:128
  103.5 9.9 %shard_map.78 = bf16[8,512,640]{2,1,0:T(8,128)(2,1)} custom-call(bf16[512,640]{1,0:T(8,128)(2,1)} %fusion.1.refs_0_, bf16[5120,640]{1,0:T(8,128)(2,1)} %bitcast.31), custom_call_target="tpu_custom_call" | custom-call | flops 3355443200 | bytes 12451840 | tf_op jit(solution)/shard_map/pallas_call | solution.py:102
  113.4 0.0 reduce-scatter.2.cloned.1.call-update
  113.4 41.1 %reduce-scatter.2.cloned.1.call-done = bf16[1,512,640]{2,1,0:T(8,128)(2,1)} async-done(((bf16[8,512,640]{2,1,0:T(8,128)(2,1)}), bf16[1,512,640]{2,1,0:T(8,128)(2,1)}) %reduce-scatter.2.cloned.1.call-update) | async-done | bytes 655376 | tf_op jit(solution)/shard_map/reduce_scatter | solution.py:141
Async XLA Ops:
  7.2 96.3 %all-gather.2.cloned.1.call-start = ((), (), s32[]{:S(2)}) async-start(), calls=%async_computation.1 | async-start | bytes 6758400 | tf_op jit(solution)/shard_map/all_gather | solution.py:128
  7.9 146.7 %reduce-scatter.2.cloned.1.call-start = ((), (), s32[]{:S(2)}) async-start(), calls=%async_computation.2 | async-start | bytes 5898240 | tf_op jit(solution)/shard_map/reduce_scatter | solution.py:141
  48.2 8.8 %copy-start.1 = (s32[4,8]{1,0:T(4,128)S(1)}, s32[4,8]{1,0:T(4,128)}, u32[]{:S(2)}) copy-start(s32[4,8]{1,0:T(4,128)} %param.8) | copy-start | bytes 388
  48.2 8.9 %copy-start = (bf16[32,128,128]{2,1,0:T(8,128)(2,1)S(1)}, bf16[32,128,128]{2,1,0:T(8,128)(2,1)}, u32[]{:S(2)}) copy-start(bf16[32,128,128]{2,1,0:T(8,128)(2,1)} %shard_map.77) | copy-start | bytes 3145732
  48.2 8.8 %copy-start.2 = (s32[32]{0:T(128)S(1)}, s32[32]{0:T(128)}, u32[]{:S(2)}) copy-start(s32[32]{0:T(128)} %param.9) | copy-start | bytes 388
Sparse Core Ops, SparseCore 0:
  10.6 92.8 all-gather.1
  113.6 40.9 reduce-scatter.1

commit v16 on v11

--- a/solution.py
+++ b/solution.py
@@ -84,7 +84,7 @@
     blocks, heads, topk = cached_probs.shape[:3]
     return pl.pallas_call(
         _refresh_kernel,
-        out_shape=jax.ShapeDtypeStruct(out_old.shape, out_old.dtype),
+        out_shape=jax.ShapeDtypeStruct(out_old.shape, jnp.float32),
         grid=(blocks, heads),
         in_specs=[
             pl.BlockSpec((1, 1, topk, BLK, BLK), lambda q, h: (q, h, 0, 0, 0)),
@@ -113,7 +113,7 @@
     onehot = (flat_lists[:, None] == changed_block_numbers[None, :]).astype(jnp.bfloat16)
     selected = jnp.dot(onehot, every_change, preferred_element_type=jnp.float32)
     picked = selected.astype(jnp.bfloat16).reshape(blocks_here, topk_here, BLK, values_here * HD)
-    attn_new = refresh(cached_probs, picked, out_old)
+    attn_new = refresh(cached_probs, picked, out_old).astype(jnp.bfloat16)
     n_head = w_full.shape[1] // attn_new.shape[1]
     w_groups = w_full.reshape(w_full.shape[0], n_head, attn_new.shape[1])
     terms = jnp.einsum("tk,kgc->gtc", attn_new, w_groups, preferred_element_type=jnp.float32)

time: 160 us -> 160 us (level)
    all_gather x1, waiting for transfers between devices: 36.8 us -> 35.2 us  [local(): w_full = lax.all_gather(w_out, 'seq', axis=1, tiled=True)]
  transfers between devices with their start and end apart: 2 -> 2, of which waited for: 2 -> 2; matrix products, arithmetic and copies ran while one was open for 2% -> 3% of each run, Pallas kernels for 34% -> 34%
where the time goes in v16:
time: 160 us; the launch traced here: 159 us
  waiting for transfers between devices  77 us (48%)
  Pallas kernels  53.7 us (34%)
  between operations  14.1 us (9%)
  matrix products  10.8 us (7%)
  local copies, waits for them, and re-layouts  2.09 us (1%)
    reduce_scatter x1, waiting for transfers between devices, local(): lax.psum_scatter(terms.astype(jnp.bfloat16), 'head', scatter_dimension=0,...  41.1 us
    pallas_call x1, Pallas kernels, gather_seq(): pl.pallas_call(lambda *refs: _gather_kernel(nx, nz, *refs), out_shape=jax...  39.8 us
    all_gather x1, waiting for transfers between devices, local(): w_full = lax.all_gather(w_out, 'seq', axis=1, tiled=True)  35.2 us
    pallas_call x1, Pallas kernels, refresh(): pl.pallas_call(_refresh_kernel, out_shape=jax.ShapeDtypeStruct(out_old.sh...  13.9 us
    dot_general x1, matrix products, local(): jnp.einsum('tk,kgc->gtc', attn_new, w_groups, preferred_element_type=jnp....  8.86 us
  transfers between devices with their start and end apart: 2, of which 2 were waited for; matrix products, arithmetic and copies ran while one was open for 3% of the time, Pallas kernels for 34%

profile of v16, /device:TPU:2, one launch (start us, length us, event | category | flops | bytes accessed | tf_op | source)
XLA Modules:
  0.0 159.2 jit_solution(14893248742373764889)
XLA Ops:
  7.2 0.0 all-gather.2.cloned.1.call-start
  7.2 0.7 all-gather.2.cloned.1.call-update
  7.9 0.0 reduce-scatter.2.cloned.1.call-start
  7.9 0.8 eq.15
  8.7 39.8 %shard_map.77 = bf16[32,128,128]{2,1,0:T(8,128)(2,1)} custom-call(bf16[128,128]{1,0:T(8,128)(2,1)} %refs_0_.1), custom_call_target="tpu_custom_call" | custom-call | tf_op jit(solution)/shard_map/pallas_call | solution.py:60
  48.6 2.0 %fusion = bf16[4,8,128,128]{3,1,2,0:T(8,128)(2,1)S(1)} fusion(bf16[4,8,128,128]{3,2,1,0:T(8,128)(2,1)} %bitcast.18, s32[32]{0:T(128)} %param.9, s32[32]{0:T(128)S(1)} %eq.15), kind=kOutput, calls=%fused_computation.2 | convolution fusion | flops 34079744 | bytes 2097408 | tf_op jit(solution)/shard_map/dot_general | solution.py:114
  50.5 1.3 copy.17
  51.9 13.9 %shard_map.78 = f32[512,640]{1,0:T(8,128)} custom-call(bf16[4,5,8,128,128]{4,3,2,1,0:T(8,128)(2,1)} %p_ref, bf16[4,8,128,128]{3,2,1,0:T(8,128)(2,1)} %copy.17, bf16[512,640]{1,0:T(8,128)(2,1)} %o_ref.1), custom_call_target="tpu_custom_call" | custom-call | flops 671088640 | bytes 7602176 | tf_op jit(solution)/shard_map/pallas_call | solution.py:85
  65.8 1.4 convert_element_type.14
  67.1 0.0 copy-start
  67.2 35.2 %all-gather.2.cloned.1.call-done = bf16[640,5120]{0,1:T(8,128)(2,1)} async-done(((bf16[640,160]{0,1:T(8,128)(2,1)}), bf16[640,5120]{0,1:T(8,128)(2,1)}) %all-gather.2.cloned.1.call-update) | async-done | bytes 6553616 | tf_op jit(solution)/shard_map/all_gather | solution.py:108
  102.4 8.9 %convert_bitcast_fusion = bf16[8,512,640]{2,1,0:T(8,128)(2,1)} fusion(bf16[640,8,640]{0,2,1:T(8,128)(2,1)} %bitcast.19, bf16[512,640]{1,0:T(8,128)(2,1)S(1)} %convert_element_type.14), kind=kOutput, calls=%fused_computation.1 | convolution fusion | flops 3358064640 | bytes 12451840 | tf_op jit(solution)/shard_map/tk,kgc->gtc/dot_general | solution.py:119
  111.2 0.0 copy-done
  111.2 0.0 reduce-scatter.2.cloned.1.call-update
  111.2 41.1 %reduce-scatter.2.cloned.1.call-done = bf16[1,512,640]{2,1,0:T(8,128)(2,1)} async-done(((bf16[8,512,640]{2,1,0:T(8,128)(2,1)}), bf16[1,512,640]{2,1,0:T(8,128)(2,1)}) %reduce-scatter.2.cloned.1.call-update) | async-done | bytes 655376 | tf_op jit(solution)/shard_map/reduce_scatter | solution.py:120
Async XLA Ops:
  7.2 95.2 %all-gather.2.cloned.1.call-start = ((), (), s32[]{:S(2)}) async-start(), calls=%async_computation.1 | async-start | bytes 6758400 | tf_op jit(solution)/shard_map/all_gather | solution.py:108
  7.9 144.4 %reduce-scatter.2.cloned.1.call-start = ((), (), s32[]{:S(2)}) async-start(), calls=%async_computation.2 | async-start | bytes 5898240 | tf_op jit(solution)/shard_map/reduce_scatter | solution.py:120
  67.1 44.1 %copy-start = (bf16[512,640]{1,0:T(8,128)(2,1)}, bf16[512,640]{1,0:T(8,128)(2,1)S(1)}, u32[]{:S(2)}) copy-start(bf16[512,640]{1,0:T(8,128)(2,1)S(1)} %convert_element_type.14) | copy-start | bytes 1966084
Sparse Core Ops, SparseCore 0:
  10.6 91.7 all-gather.1
  111.4 40.9 reduce-scatter.1
